TPU v7x, 128 devices: a whole 4x4x4 slice. The times are simulated.
128 devices in a mesh: dom: 32 (over z, x, core), dir: 4 (over y).
Axes of the slice: x: 4, y: 4, z: 4, core: 2. Of those that a mesh axis runs over, the one named last changes fastest.
Arguments:
- x_edges: bfloat16 [262144, 128], P(('dom', 'dir')), may hold values from -6 to 6
- send_list: int32 [16384, 32], P(('dom', 'dir')), may hold values from 0 to 2048, as said below
- connectivity: int32 [6, 131072], P(None, ('dom', 'dir')), may hold values from 0 to 6143, as said below
- elem_mats: float32 [36, 131072], P(None, ('dom', 'dir'))
- elem_live: int32 [128], P(('dom', 'dir')), may hold values from 512 to 1024, as said below
- currents: bfloat16 [4096, 128, 128], P(('dom', 'dir')), may hold values from -0.1796875 to 0.1796875
- positions: bfloat16 [4096, 3, 128], P(('dom', 'dir')), may hold values from -1 to 1
- block_live: int32 [4096], P(('dom', 'dir')), may hold values from 32 to 128
- block_owner: int32 [4096], P(('dom', 'dir')), may hold values from 0 to 31, as said below
- block_leaf: int32 [4096], P(('dom', 'dir')), may hold values from 0 to 15
- cone_waves: float32 [3, 16], P(None, 'dir'), may hold values from -6 to 6
Outputs:
- interior_out: float32 [262144, 128], P(('dom', 'dir'))
- expansions: float32 [64, 16, 2, 64, 128], P('dom', 'dir')
Inputs may be any that keep to these rules, and one draw needn't show every extreme that they name: `send_list`: in row a * 128 + b the used entries come first and name owned edges of a; the rest are 2048. A partition reads nothing of itself; some pair uses all 32 entries. `connectivity`: entries below 2048 are owned edges; 2048 + p * 32 + s names the s-th edge that partition p lists for this partition, and only used entries are named. `elem_live`: elements at positions from this count on are padding; some partition has all 1024. `block_owner`: among the 32 blocks of one partition at most 3 name one leaf owner; some leaf owner is named by exactly 3 blocks of every partition.
All inputs are finite; a program needn't handle non-finite values.
Results may differ from a plain program's by a relative error of at most 0.0056.
Values may be sent and summed in bfloat16 or wider, within the bound.
No kernel may reach another device: no remote copies, remote signals or barrier semaphores. Data moves between devices by JAX's collectives and lax.ppermute only.
A program may use at most 128 MiB of HBM per device.

v0:
```python
import jax
import jax.numpy as jnp
from jax import lax
from jax.sharding import PartitionSpec as P

LEAVES_DEV = 16
NODES = 4


def side_by_side(arrays, axis, split_dim, concat_dim, along):
    ends, at = ([], 0)
    for a in arrays[:-1]:
        at += a.shape[along]
        ends.append(at)
    both = jnp.concatenate(arrays, axis=along)
    return tuple(
        jnp.split(
            lax.all_to_all(both, axis, split_axis=split_dim, concat_axis=concat_dim, tiled=True),
            ends,
            axis=along,
        )
    )


def in_one_piece(arrays, axis, dim, along):
    ends, at = ([], 0)
    for a in arrays[:-1]:
        at += a.shape[along]
        ends.append(at)
    both = jnp.concatenate(arrays, axis=along)
    return tuple(jnp.split(lax.all_gather(both, axis, axis=dim, tiled=True), ends, axis=along))


def cheb_points():
    node_order = jnp.arange(NODES).astype(jnp.float32)
    return jnp.cos((2.0 * node_order + 1.0) * (jnp.pi / (2.0 * NODES)))


def lagrange(points):
    node_values = cheb_points()
    rows_out = []
    for target in range(NODES):
        product = jnp.ones_like(points)
        for other_node in range(NODES):
            if other_node != target:
                product = (
                    product
                    * (points - node_values[other_node])
                    / (node_values[target] - node_values[other_node])
                )
        rows_out.append(product)
    return jnp.stack(rows_out, axis=-2)


def tensor_basis(coords):
    first = lagrange(coords[..., 0, :])
    second = lagrange(coords[..., 1, :])
    third = lagrange(coords[..., 2, :])
    joined = (
        first[..., :, None, None, :] * second[..., None, :, None, :] * third[..., None, None, :, :]
    )
    return joined.reshape(coords.shape[:-2] + (NODES**3, coords.shape[-1]))


def node_coords():
    ladder = jnp.arange(NODES**3)
    digits = jnp.stack([ladder // (NODES * NODES), ladder // NODES % NODES, ladder % NODES]).astype(
        jnp.float32
    )
    return jnp.cos((2.0 * digits + 1.0) * (jnp.pi / (2.0 * NODES)))


def wave_phase(waves, coords):
    return (
        waves[0][:, None] * coords[..., None, 0, :]
        + waves[1][:, None] * coords[..., None, 1, :]
        + waves[2][:, None] * coords[..., None, 2, :]
    )


def m2m_tables(waves):
    octant = jnp.arange(8)
    shifts = jnp.stack([octant // 4, octant // 2 % 2, octant % 2], axis=1).astype(jnp.float32) - 0.5
    points = shifts[:, :, None] + 0.5 * cheb_points()[None, None, :]
    weights = lagrange(points)
    first = weights[:, 0]
    second = weights[:, 1]
    third = weights[:, 2]
    joined = (
        first[:, :, None, None, :, None, None]
        * second[:, None, :, None, None, :, None]
        * third[:, None, None, :, None, None, :]
    )
    square = NODES**3
    joined = joined.reshape(8, square, square)
    child = shifts[:, :, None] + 0.5 * node_coords()[None]
    spread = child[:, :, None, :] - node_coords()[None, :, :, None]
    psi = 2.0 * (
        waves[0][:, None, None, None] * spread[None, :, 0]
        + waves[1][:, None, None, None] * spread[None, :, 1]
        + waves[2][:, None, None, None] * spread[None, :, 2]
    )
    table_real = (joined[None] * jnp.cos(psi)).astype(jnp.bfloat16)
    table_imag = (-joined[None] * jnp.sin(psi)).astype(jnp.bfloat16)
    return (table_real, table_imag)


def pack_slots(owners, dest_count, capacity, members):
    matches = (owners[:, None] == jnp.arange(dest_count)[None, :]).astype(jnp.int32)
    ranking = jnp.sum((jnp.cumsum(matches, axis=0) - matches) * matches, axis=1)
    slot_index = owners * capacity + ranking
    source_row = (
        jnp.full((dest_count * capacity,), owners.shape[0], jnp.int32)
        .at[slot_index]
        .set(jnp.arange(owners.shape[0], dtype=jnp.int32))
    )
    padded = [
        jnp.concatenate([member, jnp.zeros((1,) + member.shape[1:], member.dtype)])
        for member in members
    ]
    return tuple((array_now[source_row] for array_now in padded))


def interior_part(x_edges, send_list, connectivity, elem_mats, elem_live):
    owned_rows, columns = x_edges.shape
    partitions, slot_width = send_list.shape
    element_count = connectivity.shape[1]
    padded = jnp.concatenate([x_edges, jnp.zeros((1, columns), x_edges.dtype)])
    outgoing = padded[send_list]
    received = lax.all_to_all(outgoing, ("dom", "dir"), split_axis=0, concat_axis=0, tiled=True)
    edge_table = jnp.concatenate([x_edges, received.reshape(partitions * slot_width, columns)])
    gathered = edge_table[connectivity]
    live_mask = (jnp.arange(element_count) < elem_live[0])[:, None]
    term_list = []
    for row_index in range(6):
        summed = jnp.zeros((element_count, columns), jnp.float32)
        for col_index in range(6):
            summed = summed + elem_mats[row_index * 6 + col_index][:, None] * gathered[col_index]
        term_list.append(jnp.where(live_mask, summed, jnp.zeros_like(summed)))
    stacked = jnp.stack(term_list).reshape(6 * element_count, columns)
    assembled = jax.ops.segment_sum(
        stacked, connectivity.reshape(-1), num_segments=owned_rows + partitions * slot_width
    )
    back_terms = assembled[owned_rows:]
    returned = lax.all_to_all(
        back_terms.reshape(partitions, slot_width, columns),
        ("dom", "dir"),
        split_axis=0,
        concat_axis=0,
        tiled=True,
    )
    folded = jax.ops.segment_sum(
        returned.reshape(-1, columns), send_list.reshape(-1), num_segments=owned_rows + 1
    )
    return assembled[:owned_rows] + folded[:owned_rows]


def expand_leaves(arrived_blocks, arrived_meta, waves):
    block_size = arrived_blocks.shape[1]
    columns = arrived_blocks.shape[2]
    cone_count = waves.shape[1]
    square = NODES**3
    group_rows = 512 // cone_count
    group_count = arrived_blocks.shape[0] // group_rows
    leaf_ids = arrived_meta[:, 3, 0].astype(jnp.int32)

    def one_group(carry, inputs):
        real_sum, imag_sum = carry
        blocks_now, coords, leaves = inputs
        coords_wide = coords.astype(jnp.float32)
        basis_now = tensor_basis(coords_wide)
        phase_now = wave_phase(waves, coords_wide)
        real_w = (basis_now[:, None] * jnp.cos(phase_now)[:, :, None, :]).astype(jnp.bfloat16)
        imag_w = (-basis_now[:, None] * jnp.sin(phase_now)[:, :, None, :]).astype(jnp.bfloat16)
        real_part = jnp.einsum(
            "gcqb,gbn->gcqn", real_w, blocks_now, preferred_element_type=jnp.float32
        ).astype(jnp.bfloat16)
        imag_part = jnp.einsum(
            "gcqb,gbn->gcqn", imag_w, blocks_now, preferred_element_type=jnp.float32
        ).astype(jnp.bfloat16)
        selector = (jnp.arange(LEAVES_DEV)[:, None] == leaves[None, :]).astype(jnp.bfloat16)
        real_sum = real_sum + jnp.einsum(
            "lg,gcqn->lcqn", selector, real_part, preferred_element_type=jnp.float32
        )
        imag_sum = imag_sum + jnp.einsum(
            "lg,gcqn->lcqn", selector, imag_part, preferred_element_type=jnp.float32
        )
        return ((real_sum, imag_sum), None)

    empty = jnp.zeros((LEAVES_DEV, cone_count, square, columns), jnp.float32)
    inputs = (
        arrived_blocks.reshape(group_count, group_rows, block_size, columns),
        arrived_meta[:, :3].reshape(group_count, group_rows, 3, block_size),
        leaf_ids.reshape(group_count, group_rows),
    )
    sums, unused = lax.scan(one_group, (empty, empty), inputs)
    real_sum, imag_sum = sums
    node_phase = wave_phase(waves, node_coords())
    cosine = jnp.cos(node_phase)[None, :, :, None]
    sine_part = jnp.sin(node_phase)[None, :, :, None]
    leaf_real = (cosine * real_sum - sine_part * imag_sum).astype(jnp.bfloat16)
    leaf_imag = (cosine * imag_sum + sine_part * real_sum).astype(jnp.bfloat16)
    table_real, table_imag = m2m_tables(waves)
    child_real = leaf_real.reshape(LEAVES_DEV // 8, 8, cone_count, square, columns)
    child_imag = leaf_imag.reshape(LEAVES_DEV // 8, 8, cone_count, square, columns)
    parent_real = jnp.einsum(
        "cops,xocsn->xcpn", table_real, child_real, preferred_element_type=jnp.float32
    ) - jnp.einsum("cops,xocsn->xcpn", table_imag, child_imag, preferred_element_type=jnp.float32)
    parent_imag = jnp.einsum(
        "cops,xocsn->xcpn", table_real, child_imag, preferred_element_type=jnp.float32
    ) + jnp.einsum("cops,xocsn->xcpn", table_imag, child_real, preferred_element_type=jnp.float32)
    return jnp.stack([parent_real, parent_imag], axis=2)


def boundary_part(currents, positions, block_live, block_owner, block_leaf, cone_waves):
    block_count, block_size, columns = currents.shape
    dom_count = lax.axis_size("dom")
    capacity = 3 * block_count // dom_count
    live_mask = jnp.arange(block_size)[None, :] < block_live[:, None]
    masked = jnp.where(live_mask[:, :, None], currents, jnp.zeros_like(currents))
    leaf_row = jnp.broadcast_to(
        block_leaf.astype(jnp.bfloat16)[:, None, None], (block_count, 1, block_size)
    )
    described = jnp.concatenate([positions, leaf_row], axis=1)
    packed_blocks, packed_meta = pack_slots(block_owner, dom_count, capacity, (masked, described))
    owner_blocks, owner_meta = side_by_side((packed_blocks, packed_meta), "dom", 0, 0, 1)
    arrived_blocks, arrived_meta = in_one_piece((owner_blocks, owner_meta), "dir", 0, 1)
    parents = expand_leaves(arrived_blocks, arrived_meta, cone_waves)
    return parents


def shards(
    x_edges,
    send_list,
    connectivity,
    elem_mats,
    elem_live,
    currents,
    positions,
    block_live,
    block_owner,
    block_leaf,
    cone_waves,
):
    interior_out = interior_part(x_edges, send_list, connectivity, elem_mats, elem_live)
    expansions = boundary_part(currents, positions, block_live, block_owner, block_leaf, cone_waves)
    return (interior_out, expansions)


def solution(mesh):
    placed = (
        P(("dom", "dir"), None),
        P(("dom", "dir"), None),
        P(None, ("dom", "dir")),
        P(None, ("dom", "dir")),
        P(("dom", "dir")),
        P(("dom", "dir"), None, None),
        P(("dom", "dir"), None, None),
        P(("dom", "dir")),
        P(("dom", "dir")),
        P(("dom", "dir")),
        P(None, "dir"),
    )
    return jax.shard_map(
        shards,
        mesh=mesh,
        in_specs=placed,
        out_specs=(P(("dom", "dir"), None), P("dom", "dir", None, None, None)),
        check_vma=False,
    )
```

profile of v0, /device:TPU:1, one launch (start us, length us, event | category | flops | bytes accessed | tf_op | source)
XLA Modules:
  0.0 535.8 jit_solution(9250361343820484653)
XLA Ops:
  20.0 51.3 %all_to_all.15 = bf16[96,132,128]{2,1,0:T(8,128)(2,1)S(1)} all-to-all(bf16[96,132,128]{2,1,0:T(8,128)(2,1)S(1)} %pad_maximum_fusion.3), channel_id=1, replica_groups=mesh['dom'=32,'dir'=4] {'dom'}, dimensions={0} | all-to-all | bytes 6488064 | tf_op jit(solution)/shard_map/all_to_all | solution.py:18
  74.8 15.0 %gather_fusion = bf16[4096,128]{1,0:T(8,128)(2,1)} fusion(bf16[2049,128]{1,0:T(8,128)(2,1)S(1)} %concatenate.31, s32[4096]{0:T(1024)S(1)} %broadcast_clamp_fusion.1), kind=kCustom, calls=%fused_computation | custom fusion | bytes 2113536 | tf_op jit(solution)/shard_map/gather | solution.py:129
  89.8 5.8 %all-to-all-start = ((bf16[128,32,128]{2,1,0:T(8,128)(2,1)}), bf16[128,32,128]{2,1,0:T(8,128)(2,1)S(1)}, u32[]{:S(2)}, u32[]{:S(2)}) async-start(bf16[128,32,128]{2,1,0:T(8,128)(2,1)} %bitcast.2), calls=%async_computation | async-start | bytes 2097152 | tf_op jit(solution)/shard_map/all_to_all | solution.py:130
  116.2 18.1 %gather_fusion.1 = bf16[6144,128]{1,0:T(8,128)(2,1)S(1)} fusion(bf16[6144,128]{1,0:T(8,128)(2,1)S(1)} %pad_maximum_fusion.4, s32[6144]{0:T(1024)S(1)} %broadcast_clamp_fusion), kind=kCustom, calls=%fused_computation.1 | custom fusion | bytes 3170304 | tf_op jit(solution)/shard_map/gather | solution.py:132
  143.3 34.3 %scatter_custom_fusion = f32[6144,128]{1,0:T(8,128)S(1)} fusion(s32[6144]{0:T(1024)S(1)} %reshape.1056, f32[6144,128]{1,0:T(8,128)} %bitcast.294, f32[]{:T(128)} %constant.151.clone.1), kind=kCustom, calls=%fused_computation.63 | custom fusion | flops 786432 | bytes 3146240 | tf_op jit(solution)/shard_map/scatter-add | solution.py:141
  179.8 9.5 %all-to-all-start.1 = ((f32[128,32,128]{2,1,0:T(8,128)}), f32[128,32,128]{2,1,0:T(8,128)}, u32[]{:S(2)}, u32[]{:S(2)}) async-start(f32[128,32,128]{2,1,0:T(8,128)} %bitcast.292), calls=%async_computation.1 | async-start | bytes 4194304 | tf_op jit(solution)/shard_map/all_to_all | solution.py:145
  191.3 3.2 neg.16
  194.6 3.3 copy.61
  198.0 3.3 copy.63
  203.4 19.9 %all-to-all-done.1 = f32[128,32,128]{2,1,0:T(8,128)} async-done(((f32[128,32,128]{2,1,0:T(8,128)}), f32[128,32,128]{2,1,0:T(8,128)}, u32[]{:S(2)}, u32[]{:S(2)}) %all-to-all-start.1) | async-done | bytes 2097184 | tf_op jit(solution)/shard_map/all_to_all | solution.py:145
  223.3 28.4 %scatter_custom_fusion.1 = f32[2049,128]{1,0:T(8,128)S(1)} fusion(s32[4096]{0:T(1024)S(1)} %reshape.1064, f32[4096,128]{1,0:T(8,128)} %bitcast.53, f32[]{:T(128)} %constant.151.clone.1), kind=kCustom, calls=%fused_computation.117 | custom fusion | flops 524288 | bytes 1049600 | tf_op jit(solution)/shard_map/scatter-add | solution.py:152
  255.1 11.9 %split.3 = bf16[384,128,128]{2,0,1:T(8,128)(2,1)} slice(bf16[384,132,128]{2,0,1:T(8,128)(2,1)} %all-gather.2.cloned.1.call-done), slice={[0:384], [0:128], [0:128]} | slice | bytes 25165824 | tf_op jit(solution)/shard_map/split | solution.py:31
  267.1 243.1 %while.13 = (s32[]{:T(128)}, f32[16,4,64,128]{3,0,2,1:T(8,128)S(1)}, f32[16,4,64,128]{3,0,2,1:T(8,128)}, s32[3,128]{1,0:T(4,128)S(1)}, bf16[3,128,3,128]{3,1,0,2...) while((s32[]{:T(128)}, ...), condition=%wide.region_6.7_spmd.clone, body=%wide.region_5.6_spmd.clone.sunk | while | flops 2447904768 | bytes 172591888 | solution.py:196
  312.3 4.0 constant_dynamic-slice_fusion.3
  318.5 11.7 %fusion.140 = bf16[128,4,64,128]{3,2,1,0:T(8,128)(2,1)} fusion(f32[128,4,128]{2,1,0:T(4,128)S(1)} %get-tuple-element.273, f32[128,64,128]{2,1,0:T(8,128)S(1)} %bitcast.288, bf16[1,128,128,128]{3,1,0,2:T(8,128)(2,1)S(1)} %constant_dynamic-slice_fusion.3), kind=kOutput, calls=%fused_computation.20.clone.1 | convolution fusion | flops 1086324736 | bytes 17039360 | tf_op jit(solution)/shard_map/while/body/eval_jaxpr/gcqb,gbn->gcqn/dot_general | solution.py:175
  330.2 8.2 %select_add_fusion.4 = f32[16,4,64,128]{3,0,2,1:T(8,128)S(1)} fusion(f32[16,4,64,128]{3,0,2,1:T(8,128)S(1)} %get-tuple-element.299, bf16[128,4,64,128]{3,2,1,0:T(8,128)(2,1)} %fusion.140, pred[]{:T(512)S(6)} %compare.55, s32[128]{0:T(128)S(1)} %fusion.141), kind=kOutput, calls=%fused_computation.23.clone.1 | convolution fusion | flops 135268352 | bytes 12583425 | tf_op jit(solution)/shard_map/while/body/eval_jaxpr/lg,gcqn->lcqn/dot_general | solution.py:182
  341.9 9.6 %fusion.142 = bf16[128,4,64,128]{3,2,1,0:T(8,128)(2,1)S(1)} fusion(f32[128,4,128]{2,1,0:T(4,128)S(1)} %get-tuple-element.288, f32[128,64,128]{2,1,0:T(8,128)S(1)} %neg.19, bf16[1,128,128,128]{3,1,0,2:T(8,128)(2,1)S(1)} %copy-done.1), kind=kOutput, calls=%fused_computation.19.clone.1 | convolution fusion | flops 1086324736 | bytes 17039360 | tf_op jit(solution)/shard_map/while/body/eval_jaxpr/gcqb,gbn->gcqn/dot_general | solution.py:178
  351.6 6.0 %select_add_fusion.5 = f32[16,4,64,128]{3,0,2,1:T(8,128)} fusion(f32[16,4,64,128]{3,0,2,1:T(8,128)} %get-tuple-element.300, bf16[128,4,64,128]{3,2,1,0:T(8,128)(2,1)S(1)} %fusion.142, pred[]{:T(512)S(6)} %compare.55, s32[128]{0:T(128)S(1)} %fusion.141), kind=kOutput, calls=%fused_computation.22.clone.1 | convolution fusion | flops 135268352 | bytes 12583425 | tf_op jit(solution)/shard_map/while/body/eval_jaxpr/lg,gcqn->lcqn/dot_general | solution.py:185
  386.7 4.0 constant_dynamic-slice_fusion.3
  392.8 11.7 %fusion.140 = bf16[128,4,64,128]{3,2,1,0:T(8,128)(2,1)} fusion(f32[128,4,128]{2,1,0:T(4,128)S(1)} %get-tuple-element.273, f32[128,64,128]{2,1,0:T(8,128)S(1)} %bitcast.288, bf16[1,128,128,128]{3,1,0,2:T(8,128)(2,1)S(1)} %constant_dynamic-slice_fusion.3), kind=kOutput, calls=%fused_computation.20.clone.1 | convolution fusion | flops 1086324736 | bytes 17039360 | tf_op jit(solution)/shard_map/while/body/eval_jaxpr/gcqb,gbn->gcqn/dot_general | solution.py:175
  404.5 8.2 %select_add_fusion.4 = f32[16,4,64,128]{3,0,2,1:T(8,128)S(1)} fusion(f32[16,4,64,128]{3,0,2,1:T(8,128)S(1)} %get-tuple-element.299, bf16[128,4,64,128]{3,2,1,0:T(8,128)(2,1)} %fusion.140, pred[]{:T(512)S(6)} %compare.55, s32[128]{0:T(128)S(1)} %fusion.141), kind=kOutput, calls=%fused_computation.23.clone.1 | convolution fusion | flops 135268352 | bytes 12583425 | tf_op jit(solution)/shard_map/while/body/eval_jaxpr/lg,gcqn->lcqn/dot_general | solution.py:182
  416.3 9.6 %fusion.142 = bf16[128,4,64,128]{3,2,1,0:T(8,128)(2,1)S(1)} fusion(f32[128,4,128]{2,1,0:T(4,128)S(1)} %get-tuple-element.288, f32[128,64,128]{2,1,0:T(8,128)S(1)} %neg.19, bf16[1,128,128,128]{3,1,0,2:T(8,128)(2,1)S(1)} %copy-done.1), kind=kOutput, calls=%fused_computation.19.clone.1 | convolution fusion | flops 1086324736 | bytes 17039360 | tf_op jit(solution)/shard_map/while/body/eval_jaxpr/gcqb,gbn->gcqn/dot_general | solution.py:178
  425.9 7.8 %select_add_fusion.5 = f32[16,4,64,128]{3,0,2,1:T(8,128)} fusion(f32[16,4,64,128]{3,0,2,1:T(8,128)} %get-tuple-element.300, bf16[128,4,64,128]{3,2,1,0:T(8,128)(2,1)S(1)} %fusion.142, pred[]{:T(512)S(6)} %compare.55, s32[128]{0:T(128)S(1)} %fusion.141), kind=kOutput, calls=%fused_computation.22.clone.1 | convolution fusion | flops 135268352 | bytes 12583425 | tf_op jit(solution)/shard_map/while/body/eval_jaxpr/lg,gcqn->lcqn/dot_general | solution.py:185
  462.8 4.0 constant_dynamic-slice_fusion.3
  468.9 11.7 %fusion.140 = bf16[128,4,64,128]{3,2,1,0:T(8,128)(2,1)} fusion(f32[128,4,128]{2,1,0:T(4,128)S(1)} %get-tuple-element.273, f32[128,64,128]{2,1,0:T(8,128)S(1)} %bitcast.288, bf16[1,128,128,128]{3,1,0,2:T(8,128)(2,1)S(1)} %constant_dynamic-slice_fusion.3), kind=kOutput, calls=%fused_computation.20.clone.1 | convolution fusion | flops 1086324736 | bytes 17039360 | tf_op jit(solution)/shard_map/while/body/eval_jaxpr/gcqb,gbn->gcqn/dot_general | solution.py:175
  480.6 8.2 %select_add_fusion.4 = f32[16,4,64,128]{3,0,2,1:T(8,128)S(1)} fusion(f32[16,4,64,128]{3,0,2,1:T(8,128)S(1)} %get-tuple-element.299, bf16[128,4,64,128]{3,2,1,0:T(8,128)(2,1)} %fusion.140, pred[]{:T(512)S(6)} %compare.55, s32[128]{0:T(128)S(1)} %fusion.141), kind=kOutput, calls=%fused_computation.23.clone.1 | convolution fusion | flops 135268352 | bytes 12583425 | tf_op jit(solution)/shard_map/while/body/eval_jaxpr/lg,gcqn->lcqn/dot_general | solution.py:182
  492.4 9.6 %fusion.142 = bf16[128,4,64,128]{3,2,1,0:T(8,128)(2,1)S(1)} fusion(f32[128,4,128]{2,1,0:T(4,128)S(1)} %get-tuple-element.288, f32[128,64,128]{2,1,0:T(8,128)S(1)} %neg.19, bf16[1,128,128,128]{3,1,0,2:T(8,128)(2,1)S(1)} %copy-done.1), kind=kOutput, calls=%fused_computation.19.clone.1 | convolution fusion | flops 1086324736 | bytes 17039360 | tf_op jit(solution)/shard_map/while/body/eval_jaxpr/gcqb,gbn->gcqn/dot_general | solution.py:178
  502.0 7.8 %select_add_fusion.5 = f32[16,4,64,128]{3,0,2,1:T(8,128)} fusion(f32[16,4,64,128]{3,0,2,1:T(8,128)} %get-tuple-element.300, bf16[128,4,64,128]{3,2,1,0:T(8,128)(2,1)S(1)} %fusion.142, pred[]{:T(512)S(6)} %compare.55, s32[128]{0:T(128)S(1)} %fusion.141), kind=kOutput, calls=%fused_computation.22.clone.1 | convolution fusion | flops 135268352 | bytes 12583425 | tf_op jit(solution)/shard_map/while/body/eval_jaxpr/lg,gcqn->lcqn/dot_general | solution.py:185
  512.4 3.8 convolution_bitcast_fusion
  516.3 3.8 convolution_bitcast_fusion.2
  520.1 3.8 fusion.29
  523.9 4.0 fusion.27
  (201 shorter events, 99.2 us)
Async XLA Ops:
  7.2 246.9 %all-gather.2.cloned.1.call-start = ((), (), s32[]{:S(2)}) async-start(), calls=%async_computation.3 | async-start | bytes 16220160 | tf_op jit(solution)/shard_map/all_gather | solution.py:31
  74.7 39.8 %copy-start.14 = (s32[6,1024]{1,0:T(8,128)S(1)}, s32[6,1024]{1,0:T(8,128)}, u32[]{:S(2)}) copy-start(s32[6,1024]{1,0:T(8,128)} %param.15) | copy-start | bytes 73732
  74.8 39.9 %copy-start.13 = (f32[36,1024]{1,0:T(8,128)S(1)}, f32[36,1024]{1,0:T(8,128)}, u32[]{:S(2)}) copy-start(f32[36,1024]{1,0:T(8,128)} %param.16) | copy-start | bytes 442372
  89.8 26.3 %all-to-all-start = ((bf16[128,32,128]{2,1,0:T(8,128)(2,1)}), bf16[128,32,128]{2,1,0:T(8,128)(2,1)S(1)}, u32[]{:S(2)}, u32[]{:S(2)}) async-start(bf16[128,32,128]{2,1,0:T(8,128)(2,1)} %bitcast.2), calls=%async_computation | async-start | bytes 2097152 | tf_op jit(solution)/shard_map/all_to_all | solution.py:130
  177.5 2.3 copy-start.6
  179.8 43.5 %all-to-all-start.1 = ((f32[128,32,128]{2,1,0:T(8,128)}), f32[128,32,128]{2,1,0:T(8,128)}, u32[]{:S(2)}, u32[]{:S(2)}) async-start(f32[128,32,128]{2,1,0:T(8,128)} %bitcast.292), calls=%async_computation.1 | async-start | bytes 4194304 | tf_op jit(solution)/shard_map/all_to_all | solution.py:145
  194.6 6.8 %copy-start.17 = (f32[3,4]{1,0:T(4,128)S(1)}, f32[3,4]{1,0:T(4,128)}, u32[]{:S(2)}) copy-start(f32[3,4]{1,0:T(4,128)} %param.23) | copy-start | bytes 148
  201.4 52.7 %copy-start.20 = (f32[4]{0:T(128)}, f32[4]{0:T(128)S(1)}, u32[]{:S(2)}) copy-start(f32[4]{0:T(128)S(1)} %get-tuple-element.178) | copy-start | bytes 52
  201.4 52.7 %copy-start.22 = (f32[4]{0:T(128)}, f32[4]{0:T(128)S(1)}, u32[]{:S(2)}) copy-start(f32[4]{0:T(128)S(1)} %get-tuple-element.179) | copy-start | bytes 52
  201.4 52.7 %copy-start.24 = (f32[4]{0:T(128)}, f32[4]{0:T(128)S(1)}, u32[]{:S(2)}) copy-start(f32[4]{0:T(128)S(1)} %get-tuple-element.180) | copy-start | bytes 52
  255.1 11.9 %slice-start = ((bf16[384,132,128]{2,0,1:T(8,128)(2,1)}), bf16[384,3,128]{2,0,1:T(8,128)(2,1)S(1)}, s32[]{:S(2)}) async-start(bf16[384,132,128]{2,0,1:T(8,128)(2,1)} %all-gather.2.cloned.1.call-done), calls=%async_computation.4 | async-start | bytes 589824 | tf_op jit(solution)/shard_map/slice | solution.py:193
  267.1 243.1 %copy-start.18 = (f32[4,64]{1,0:T(4,128)S(1)}, f32[4,64]{1,0:T(4,128)}, u32[]{:S(2)}) copy-start(f32[4,64]{1,0:T(4,128)} %get-tuple-element.172) | copy-start | bytes 3076
  267.1 243.1 %copy-start.19 = (f32[4,64]{1,0:T(4,128)S(1)}, f32[4,64]{1,0:T(4,128)}, u32[]{:S(2)}) copy-start(f32[4,64]{1,0:T(4,128)} %get-tuple-element.173) | copy-start | bytes 3076
  312.3 4.1 copy-start.2
  330.2 9.6 %copy-start.3 = (f32[128,4,4,4,128]{4,3,2,1,0:T(4,128)S(1)}, f32[128,4,4,4,128]{4,3,2,1,0:T(4,128)}, u32[]{:S(2)}) copy-start(f32[128,4,4,4,128]{4,3,2,1,0:T(4,128)} %copy-done.2) | copy-start | bytes 12582916 | tf_op jit(solution)/shard_map/while
  339.7 2.2 copy-start.1
  351.6 6.0 %copy-start.5 = (f32[16,4,64,128]{3,0,2,1:T(8,128)S(1)}, f32[16,4,64,128]{3,0,2,1:T(8,128)}, u32[]{:S(2)}) copy-start(f32[16,4,64,128]{3,0,2,1:T(8,128)} %copy-done.4) | copy-start | bytes 6291460 | tf_op jit(solution)/shard_map/while
  386.7 4.1 copy-start.2
  404.5 9.6 %copy-start.3 = (f32[128,4,4,4,128]{4,3,2,1,0:T(4,128)S(1)}, f32[128,4,4,4,128]{4,3,2,1,0:T(4,128)}, u32[]{:S(2)}) copy-start(f32[128,4,4,4,128]{4,3,2,1,0:T(4,128)} %copy-done.2) | copy-start | bytes 12582916 | tf_op jit(solution)/shard_map/while
  414.1 2.2 copy-start.1
  425.9 7.8 %copy-start.5 = (f32[16,4,64,128]{3,0,2,1:T(8,128)S(1)}, f32[16,4,64,128]{3,0,2,1:T(8,128)}, u32[]{:S(2)}) copy-start(f32[16,4,64,128]{3,0,2,1:T(8,128)} %copy-done.4) | copy-start | bytes 6291460 | tf_op jit(solution)/shard_map/while
  462.7 4.1 copy-start.2
  480.6 9.6 %copy-start.3 = (f32[128,4,4,4,128]{4,3,2,1,0:T(4,128)S(1)}, f32[128,4,4,4,128]{4,3,2,1,0:T(4,128)}, u32[]{:S(2)}) copy-start(f32[128,4,4,4,128]{4,3,2,1,0:T(4,128)} %copy-done.2) | copy-start | bytes 12582916 | tf_op jit(solution)/shard_map/while
  490.2 2.2 copy-start.1
  502.0 7.8 %copy-start.5 = (f32[16,4,64,128]{3,0,2,1:T(8,128)S(1)}, f32[16,4,64,128]{3,0,2,1:T(8,128)}, u32[]{:S(2)}) copy-start(f32[16,4,64,128]{3,0,2,1:T(8,128)} %copy-done.4) | copy-start | bytes 6291460 | tf_op jit(solution)/shard_map/while
  510.2 2.2 copy-start.9
  510.2 2.2 copy-start.10
  510.2 2.2 copy-start.11
  510.2 2.2 copy-start.12
  510.2 2.2 copy-start.21
  510.2 2.2 copy-start.23
  512.3 7.8 %copy-start.8 = (f32[8,64,64]{1,0,2:T(8,128)S(1)}, f32[8,64,64]{1,0,2:T(8,128)}, u32[]{:S(2)}) copy-start(f32[8,64,64]{1,0,2:T(8,128)} %copy.61) | copy-start | bytes 393220
  (10 other events, 16.3 us)
Sparse Core Ops, SparseCore 0:
  73.6 153.0 all-gather.1
where the time goes:
time: 546 us; the launch traced here: 536 us
  other arithmetic  129 us (24%)
  matrix products  126 us (23%)
  local copies, waits for them, and re-layouts  98.1 us (18%)
  loops' own time  64.5 us (12%)
  blocking collectives  51.3 us (9%)
  between operations  30.4 us (6%)
  waiting for transfers between devices  21.2 us (4%)
  starting transfers between devices  15.3 us (3%)
    another operation x1, loops' own time, expand_leaves(): sums, unused = lax.scan(one_group, (empty, empty), inputs)  64.5 us
    all_to_all x1, blocking collectives, side_by_side(): lax.all_to_all(both, axis, split_axis=split_dim, concat_axis=concat_dim,...  51.3 us
    dot_general x3, matrix products, one_group(): jnp.einsum('gcqb,gbn->gcqn', real_w, blocks_now, preferred_element_type=j...  35.1 us
    scatter-add x1, other arithmetic, interior_part(): jax.ops.segment_sum(stacked, connectivity.reshape(-1), num_segments=owned...  34.3 us
    dot_general x3, matrix products, one_group(): jnp.einsum('gcqb,gbn->gcqn', imag_w, blocks_now, preferred_element_type=j...  28.9 us
    scatter-add x1, other arithmetic, interior_part(): jax.ops.segment_sum(returned.reshape(-1, columns), send_list.reshape(-1),...  28.4 us
    div x10, other arithmetic, lagrange(): product * (points - node_values[other_node])  26.9 us
    dot_general x3, matrix products, one_group(): jnp.einsum('lg,gcqn->lcqn', selector, real_part, preferred_element_type=j...  24.6 us
  transfers between devices with their start and end apart: 3, of which 2 were waited for; matrix products, arithmetic and copies ran while one was open for 23% of the time, Pallas kernels for 0%

commit v1 on v0

v1 whole, which is shorter than its diff:
```python
import functools
import math

import jax
import jax.numpy as jnp
from jax import lax
from jax.experimental import pallas as pl
from jax.experimental.pallas import tpu as pltpu
from jax.sharding import PartitionSpec as P

NODES = 4
SQUARE = NODES**3
DIRS = 4
ROWS = 136
VMEM_LIMIT = 60 * 1024 * 1024
NODE_T = [math.cos((2 * j + 1) * math.pi / (2 * NODES)) for j in range(NODES)]


def vmem():
    return pl.BlockSpec(memory_space=pltpu.VMEM)


def smem():
    return pl.BlockSpec(memory_space=pltpu.SMEM)


def params():
    return pltpu.CompilerParams(vmem_limit_bytes=VMEM_LIMIT)


def pick_kernel(list_ref, x_ref, out_ref, wide, picked):
    owned, columns = x_ref.shape
    count, width = list_ref.shape
    wide[0:owned, :] = x_ref[...].astype(jnp.float32)
    wide[owned : owned + 8, :] = jnp.zeros((8, columns), jnp.float32)

    def one(row, carry):
        for slot in range(width):
            picked[pl.ds(row * width + slot, 1), :] = wide[pl.ds(list_ref[row, slot], 1), :]
        return carry

    lax.fori_loop(0, count, one, 0)
    out_ref[...] = picked[...].astype(out_ref.dtype)


def pick_rows(send_list, x_edges):
    owned, columns = x_edges.shape
    total = send_list.shape[0] * send_list.shape[1]
    return pl.pallas_call(
        pick_kernel,
        out_shape=jax.ShapeDtypeStruct((total, columns), x_edges.dtype),
        in_specs=[smem(), vmem()],
        out_specs=vmem(),
        scratch_shapes=[
            pltpu.VMEM((owned + 8, columns), jnp.float32),
            pltpu.VMEM((total, columns), jnp.float32),
        ],
        compiler_params=params(),
        cost_estimate=pl.CostEstimate(flops=0, bytes_accessed=1 << 24, transcendentals=0),
        name="pick_rows",
    )(send_list, x_edges)


GROUP = 8
PAIR = 2


def element_kernel(
    conn_ref, x_ref, halo_ref, mats_ref, local_ref, back_ref, table, stage, terms, *sums
):
    owned = x_ref.shape[0]
    halo = halo_ref.shape[0]
    elements = conn_ref.shape[1]
    columns = x_ref.shape[1]
    table[0:owned, :] = x_ref[...].astype(jnp.float32)
    table[owned : owned + halo, :] = halo_ref[...].astype(jnp.float32)
    for total in sums:
        total[...] = jnp.zeros_like(total)
    split = len(sums)

    def one(step, carry):
        for part in range(PAIR):
            first = (step * PAIR + part) * GROUP
            base = part * 6 * GROUP
            for j in range(6):
                for s in range(GROUP):
                    stage[base + j * GROUP + s : base + j * GROUP + s + 1, :] = table[
                        pl.ds(conn_ref[j, first + s], 1), :
                    ]
        for part in range(PAIR):
            first = (step * PAIR + part) * GROUP
            base = part * 6 * GROUP
            coefs = mats_ref[pl.ds(pl.multiple_of(first, GROUP), GROUP), :]
            values = [stage[base + j * GROUP : base + (j + 1) * GROUP, :] for j in range(6)]
            for i in range(6):
                term = None
                for j in range(6):
                    q = i * 6 + j
                    piece = jnp.broadcast_to(coefs[:, q : q + 1], (GROUP, columns)) * values[j]
                    term = piece if term is None else term + piece
                terms[base + i * GROUP : base + (i + 1) * GROUP, :] = term
        for part in range(PAIR):
            first = (step * PAIR + part) * GROUP
            base = part * 6 * GROUP
            for s in range(GROUP):
                for i in range(6):
                    row = pl.ds(conn_ref[i, first + s], 1)
                    at = base + i * GROUP + s
                    total = sums[i % split]
                    total[row, :] = total[row, :] + terms[at : at + 1, :]
        return carry

    lax.fori_loop(0, elements // (GROUP * PAIR), one, 0)

    def finish(step, carry):
        at = pl.ds(pl.multiple_of(step * 256, 256), 256)
        whole = sums[0][at, :]
        for total in sums[1:]:
            whole = whole + total[at, :]
        local_ref[at, :] = whole
        return carry

    lax.fori_loop(0, owned // 256, finish, 0)

    def finish_back(step, carry):
        at = pl.ds(pl.multiple_of(step * 256, 256), 256)
        src = pl.ds(pl.multiple_of(owned + step * 256, 256), 256)
        whole = sums[0][src, :]
        for total in sums[1:]:
            whole = whole + total[src, :]
        back_ref[at, :] = whole.astype(back_ref.dtype)
        return carry

    lax.fori_loop(0, halo // 256, finish_back, 0)


def element_sums(connectivity, x_edges, halo, mats):
    owned, columns = x_edges.shape
    slots = halo.shape[0]
    return pl.pallas_call(
        element_kernel,
        out_shape=(
            jax.ShapeDtypeStruct((owned, columns), jnp.float32),
            jax.ShapeDtypeStruct((slots, columns), jnp.bfloat16),
        ),
        in_specs=[smem(), vmem(), vmem(), vmem()],
        out_specs=(vmem(), vmem()),
        scratch_shapes=[
            pltpu.VMEM((owned + slots, columns), jnp.float32),
            pltpu.VMEM((6 * GROUP * PAIR, columns), jnp.float32),
            pltpu.VMEM((6 * GROUP * PAIR, columns), jnp.float32),
        ]
        + [pltpu.VMEM((owned + slots, columns), jnp.float32) for _ in range(6)],
        compiler_params=params(),
        cost_estimate=pl.CostEstimate(flops=0, bytes_accessed=1 << 26, transcendentals=0),
        name="element_sums",
    )(connectivity, x_edges, halo, mats)


def fold_kernel(list_ref, returned_ref, local_ref, out_ref):
    owned = local_ref.shape[0]
    total = returned_ref.shape[0]
    tile = 256

    def one(step, carry):
        at = pl.ds(pl.multiple_of(step * tile, tile), tile)
        rows = lax.broadcasted_iota(jnp.int32, (tile, total), 0) + step * tile
        hot = jnp.where(rows == list_ref[...], 1.0, 0.0).astype(jnp.bfloat16)
        out_ref[at, :] = local_ref[at, :] + jnp.dot(
            hot, returned_ref[...], preferred_element_type=jnp.float32
        )
        return carry

    lax.fori_loop(0, owned // tile, one, 0)


def fold_back(list_row, returned, local):
    return pl.pallas_call(
        fold_kernel,
        out_shape=jax.ShapeDtypeStruct(local.shape, jnp.float32),
        in_specs=[vmem(), vmem(), vmem()],
        out_specs=vmem(),
        compiler_params=params(),
        cost_estimate=pl.CostEstimate(flops=0, bytes_accessed=1 << 24, transcendentals=0),
        name="fold_back",
    )(list_row, returned, local)


def sin_cos_turns(turns):
    reduced = turns - jnp.floor(turns + 0.5)
    half = reduced * math.pi
    square = half * half

    def series(coefs):
        total = jnp.full_like(square, coefs[-1])
        for coef in coefs[-2::-1]:
            total = total * square + coef
        return total

    sine = half * series([(-1) ** n / math.factorial(2 * n + 1) for n in range(6)])
    cosine = series([(-1) ** n / math.factorial(2 * n) for n in range(7)])
    return 2.0 * sine * cosine, 1.0 - 2.0 * sine * sine


def digit_polynomial(coords, digit):
    total = None
    for j in range(NODES):
        value = None
        for i in range(NODES):
            if i != j:
                factor = (coords - NODE_T[i]) * (1.0 / (NODE_T[j] - NODE_T[i]))
                value = factor if value is None else value * factor
        total = value if total is None else jnp.where(digit == j, value, total)
    return total


def parent_kernel(blocks_ref, waves_ref, *refs):
    outs = refs[:DIRS]
    weights, sources, sums = refs[DIRS:]
    slots, unused, columns = blocks_ref.shape
    cones = waves_ref.shape[1]
    size = columns
    per_dir = cones // DIRS
    span = sources.shape[0] // size

    lane_rows = lax.broadcasted_iota(jnp.int32, (8, size), 0)
    y_rows = lax.broadcasted_iota(jnp.int32, (size, columns), 0).astype(jnp.float32)
    third_digit = lane_rows % NODES
    second_low = lane_rows // NODES

    sums[...] = jnp.zeros_like(sums)

    def one(step, carry):
        for part in range(span):
            slot = step * span + part
            meta = blocks_ref[slot, size : size + 8, :].astype(jnp.float32)
            block = blocks_ref[slot, 0:size, :].astype(jnp.float32)
            live = jnp.broadcast_to(meta[7:8, :], (size, columns))
            parent = jnp.broadcast_to(meta[6:7, :], (size, columns))
            block = jnp.where(y_rows < live, block, 0.0)
            at = slice(part * size, (part + 1) * size)
            sources[at, 0:columns] = jnp.where(parent < 0.5, block, 0.0).astype(jnp.bfloat16)
            sources[at, columns : 2 * columns] = jnp.where(parent > 0.5, block, 0.0).astype(
                jnp.bfloat16
            )
            shifted = meta[0:3, :] + meta[3:6, :]
            turns = None
            for d in range(3):
                piece = waves_ref[d] * jnp.broadcast_to(shifted[d : d + 1, :], (cones, size))
                turns = piece if turns is None else turns + piece
            sine, cosine = sin_cos_turns(turns)
            coords = shifted * 0.5
            along = [jnp.broadcast_to(coords[d : d + 1, :], (8, size)) for d in range(3)]
            third = digit_polynomial(along[2], third_digit)
            second = [digit_polynomial(along[1], second_low + 2 * h) * third for h in range(2)]
            first = [
                digit_polynomial(along[0], jnp.full((8, size), j, jnp.int32)) for j in range(NODES)
            ]
            basis = jnp.concatenate([first[v // 2] * second[v % 2] for v in range(8)], axis=0)
            for k in range(cones):
                base = k * 2 * SQUARE
                weights[base : base + SQUARE, at] = (
                    basis * jnp.broadcast_to(cosine[k : k + 1, :], (SQUARE, size))
                ).astype(jnp.bfloat16)
                weights[base + SQUARE : base + 2 * SQUARE, at] = (
                    basis * jnp.broadcast_to(-sine[k : k + 1, :], (SQUARE, size))
                ).astype(jnp.bfloat16)
        height = 512
        for row in range(0, cones * 2 * SQUARE, height):
            sums[row : row + height, :] += jnp.dot(
                weights[row : row + height, :],
                sources[...],
                preferred_element_type=jnp.float32,
            )
        return carry

    lax.fori_loop(0, slots // span, one, 0)

    node_rows = lax.broadcasted_iota(jnp.int32, (SQUARE, columns), 0)

    def node_value(digit):
        value = jnp.full((SQUARE, columns), NODE_T[0], jnp.float32)
        for j in range(1, NODES):
            value = jnp.where(digit == j, NODE_T[j], value)
        return value

    nodes = [
        node_value(node_rows // (NODES * NODES)),
        node_value(node_rows // NODES % NODES),
        node_value(node_rows % NODES),
    ]
    for k in range(cones):
        turns = None
        for d in range(3):
            wave = jnp.broadcast_to(waves_ref[d, k : k + 1, :], (SQUARE, columns))
            piece = wave * nodes[d]
            turns = piece if turns is None else turns + piece
        sine, cosine = sin_cos_turns(2.0 * turns)
        base = k * 2 * SQUARE
        out = outs[k // per_dir]
        for p in range(2):
            cols = slice(p * columns, (p + 1) * columns)
            real = sums[base : base + SQUARE, cols]
            imag = sums[base + SQUARE : base + 2 * SQUARE, cols]
            out[p, k % per_dir, 0] = (cosine * real - sine * imag).astype(out.dtype)
            out[p, k % per_dir, 1] = (cosine * imag + sine * real).astype(out.dtype)


SPAN = 2


def parent_sums(blocks, waves):
    columns = blocks.shape[2]
    cones = waves.shape[1]
    piece = (2, cones // DIRS, 2, SQUARE, columns)
    rows = cones * 2 * SQUARE
    return pl.pallas_call(
        parent_kernel,
        out_shape=(jax.ShapeDtypeStruct(piece, jnp.float32),)
        + (jax.ShapeDtypeStruct(piece, jnp.bfloat16),) * (DIRS - 1),
        in_specs=[vmem(), vmem()],
        out_specs=(vmem(),) * DIRS,
        scratch_shapes=[
            pltpu.VMEM((rows, SPAN * 128), jnp.bfloat16),
            pltpu.VMEM((SPAN * 128, 2 * columns), jnp.bfloat16),
            pltpu.VMEM((rows, 2 * columns), jnp.float32),
        ],
        compiler_params=params(),
        cost_estimate=pl.CostEstimate(
            flops=2 * rows * 2 * columns * blocks.shape[0] * 128,
            bytes_accessed=1 << 24,
            transcendentals=0,
        ),
        name="parent_sums",
    )(blocks, waves)


def packed_blocks(currents, positions, block_live, block_owner, block_leaf):
    count, size, columns = currents.shape
    owners = lax.axis_size("dom")
    capacity = 3 * count // owners
    octant = block_leaf % 8
    digits = jnp.stack([octant // 4, octant // 2 % 2, octant % 2], axis=1)
    facts = jnp.concatenate(
        [2 * digits - 1, (block_leaf // 8)[:, None], block_live[:, None]], axis=1
    ).astype(jnp.bfloat16)
    joined = jnp.concatenate(
        [currents, positions, jnp.broadcast_to(facts[:, :, None], (count, 5, columns))], axis=1
    )
    joined = jnp.concatenate([joined, jnp.zeros((1, ROWS, columns), joined.dtype)])
    order = jnp.arange(count)
    same = (block_owner[:, None] == block_owner[None, :]) & (order[None, :] < order[:, None])
    slot = block_owner * capacity + jnp.sum(same.astype(jnp.int32), axis=1)
    hits = slot[None, :] == jnp.arange(owners * capacity)[:, None]
    source = jnp.min(jnp.where(hits, order[None, :], count), axis=1)
    return joined[source]


def shards(
    x_edges,
    send_list,
    connectivity,
    elem_mats,
    elem_live,
    currents,
    positions,
    block_live,
    block_owner,
    block_leaf,
    cone_waves,
):
    owned, columns = x_edges.shape
    partitions, width = send_list.shape
    elements = connectivity.shape[1]
    everywhere = ("dom", "dir")

    outgoing = pick_rows(send_list, x_edges).reshape(partitions, width, columns)
    halo = lax.all_to_all(outgoing, everywhere, split_axis=0, concat_axis=0, tiled=True)

    waves = [cone_waves]
    for s in range(1, DIRS):
        waves.append(
            lax.ppermute(cone_waves, "dir", [(i, (i - s) % DIRS) for i in range(DIRS)])
        )
    waves = jnp.concatenate(waves, axis=1) * (0.5 / math.pi)
    waves = jnp.broadcast_to(waves[:, :, None], waves.shape + (columns,))

    packed = packed_blocks(currents, positions, block_live, block_owner, block_leaf)
    live = jnp.arange(elements)[None, :] < elem_live[0]
    mats = jnp.where(live, elem_mats, 0.0).T
    list_row = send_list.reshape(1, partitions * width)

    halo, packed, mats, list_row = lax.optimization_barrier((halo, packed, mats, list_row))
    arrived = lax.all_to_all(packed, "dom", split_axis=0, concat_axis=0, tiled=True)
    local, back = element_sums(
        connectivity, x_edges, halo.reshape(partitions * width, columns), mats
    )
    back, arrived = lax.optimization_barrier((back, arrived))
    returned = lax.all_to_all(
        back.reshape(partitions, width, columns),
        everywhere,
        split_axis=0,
        concat_axis=0,
        tiled=True,
    )
    pieces = parent_sums(arrived, waves)
    expansions = pieces[0]
    for s in range(1, DIRS):
        moved = lax.ppermute(pieces[s], "dir", [(i, (i + s) % DIRS) for i in range(DIRS)])
        expansions = expansions + moved.astype(jnp.float32)
    interior_out = fold_back(list_row, returned.reshape(partitions * width, columns), local)
    return (interior_out, expansions)


def solution(mesh):
    both = ("dom", "dir")
    placed = (
        P(both, None),
        P(both, None),
        P(None, both),
        P(None, both),
        P(both),
        P(both, None, None),
        P(both, None, None),
        P(both),
        P(both),
        P(both),
        P(None, "dir"),
    )
    return jax.shard_map(
        shards,
        mesh=mesh,
        in_specs=placed,
        out_specs=(P(both, None), P("dom", "dir", None, None, None)),
        check_vma=False,
    )
```

time: 546 us -> 151 us (0.28); the launches traced: 536 us -> 151 us
  matrix products: 126 us -> 0 us
  other arithmetic: 129 us -> 4.74 us
  local copies, waits for them, and re-layouts: 98.1 us -> 8.14 us
  Pallas kernels: 0 us -> 66.8 us
  loops' own time: 64.5 us -> 0 us
  blocking collectives: 51.3 us -> 0 us
  between operations: 30.4 us -> 1.49 us
  waiting for transfers between devices: 21.2 us -> 38.7 us
  starting transfers between devices: 15.3 us -> 30.6 us
    dot_general x16 -> x0, matrix products: 126 us -> none  [the longest x3 35.1 us: one_group(): jnp.einsum('gcqb,gbn->gcqn', real_w, blocks_now, preferred_element_type=j...]
    pallas_call x0 -> x4, Pallas kernels: none -> 66.8 us  [the longest x1 29.3 us: parent_sums(): pl.pallas_call(parent_kernel, out_shape=(jax.ShapeDtypeStruct(piece, jnp....]
    another operation x1 -> x0, loops' own time: 64.5 us -> none  [expand_leaves(): sums, unused = lax.scan(one_group, (empty, empty), inputs)]
    scatter-add x2 -> x0, other arithmetic: 62.7 us -> none  [the longest x1 34.3 us: interior_part(): jax.ops.segment_sum(stacked, connectivity.reshape(-1), num_segments=owned...]
    all_to_all x1 -> x0, blocking collectives: 51.3 us -> none  [side_by_side(): lax.all_to_all(both, axis, split_axis=split_dim, concat_axis=concat_dim,...]
    gather x4 -> x1, local copies, waits for them, and re-layouts: 36.5 us -> 2.89 us  [packed_blocks(): return joined[source]]
    div x10 -> x0, other arithmetic: 26.9 us -> none  [lagrange(): product * (points - node_values[other_node])]
    while x36 -> x0, local copies, waits for them, and re-layouts: 15.5 us -> none
  transfers between devices with their start and end apart: 3 -> 9, of which waited for: 2 -> 6; matrix products, arithmetic and copies ran while one was open for 23% -> 6% of each run, Pallas kernels for 0% -> 34%
where the time goes in v1:
time: 151 us
  Pallas kernels  66.8 us (44%)
  waiting for transfers between devices  38.7 us (26%)
  starting transfers between devices  30.6 us (20%)
  local copies, waits for them, and re-layouts  8.14 us (5%)
  other arithmetic  4.74 us (3%)
    pallas_call x1, Pallas kernels, parent_sums(): pl.pallas_call(parent_kernel, out_shape=(jax.ShapeDtypeStruct(piece, jnp....  29.3 us
    pallas_call x1, Pallas kernels, element_sums(): pl.pallas_call(element_kernel, out_shape=(jax.ShapeDtypeStruct((owned, co...  22.4 us
    all_to_all x1, waiting for transfers between devices, shards(): lax.all_to_all(packed, 'dom', split_axis=0, concat_axis=0, tiled=True)  12 us
    all_to_all x1, waiting for transfers between devices, shards(): lax.all_to_all(outgoing, everywhere, split_axis=0, concat_axis=0, tiled=T...  11.9 us
    all_to_all x1, starting transfers between devices, shards(): lax.all_to_all(outgoing, everywhere, split_axis=0, concat_axis=0, tiled=T...  11.5 us
    ppermute x3, waiting for transfers between devices, shards(): lax.ppermute(pieces[s], 'dir', [(i, (i + s) % DIRS) for i in range(DIRS)])  10.7 us
    pallas_call x1, Pallas kernels, fold_back(): pl.pallas_call(fold_kernel, out_shape=jax.ShapeDtypeStruct(local.shape, j...  8.12 us
    pallas_call x1, Pallas kernels, pick_rows(): pl.pallas_call(pick_kernel, out_shape=jax.ShapeDtypeStruct((total, column...  6.91 us
  transfers between devices with their start and end apart: 9, of which 6 were waited for; matrix products, arithmetic and copies ran while one was open for 6% of the time, Pallas kernels for 34%

profile of v1, /device:TPU:1, one launch (start us, length us, event | category | flops | bytes accessed | tf_op | source)
XLA Modules:
  0.0 150.5 jit_solution(7383810015677663001)
XLA Ops:
  0.7 1.5 copy.23.list_ref
  2.2 6.9 %pick_rows.1 = bf16[4096,128]{1,0:T(8,128)(2,1)} custom-call(s32[128,32]{1,0:T(8,128)} %copy.23.list_ref, bf16[2048,128]{1,0:T(8,128)(2,1)} %x_ref.3), custom_call_target="tpu_custom_call" | custom-call | bytes 16777216 | tf_op jit(solution)/shard_map/pick_rows/pallas_call | solution.py:49
  9.1 11.5 %all-to-all-start = ((bf16[128,32,128]{2,1,0:T(8,128)(2,1)}), bf16[128,32,128]{2,1,0:T(8,128)(2,1)S(1)}, u32[]{:S(2)}, u32[]{:S(2)}) async-start(bf16[128,32,128]{2,1,0:T(8,128)(2,1)} %bitcast.24), calls=%async_computation | async-start | bytes 2097152 | tf_op jit(solution)/shard_map/all_to_all | solution.py:378
  20.6 0.2 convert_reduce_fusion
  20.9 0.7 reshape.106.list_ref
  22.3 0.1 copy.24
  22.4 0.2 copy.26
  22.6 0.1 select_reduce_fusion
  22.7 0.1 broadcast_in_dim.20
  22.8 1.3 fusion.4
  24.2 2.9 %gather_fusion = bf16[96,136,128]{2,1,0:T(8,128)(2,1)} fusion(bf16[33,136,128]{2,1,0:T(8,128)(2,1)S(1)} %fusion.4, s32[1024]{0:T(1024)S(1)} %pad_clamp_fusion), kind=kCustom, calls=%fused_computation | custom fusion | bytes 6685056 | tf_op jit(solution)/shard_map/gather | solution.py:356
  27.1 1.0 select_bitcast_fusion.mats_ref
  28.1 11.9 %all-to-all-done = bf16[128,32,128]{2,1,0:T(8,128)(2,1)S(1)} async-done(((bf16[128,32,128]{2,1,0:T(8,128)(2,1)}), bf16[128,32,128]{2,1,0:T(8,128)(2,1)S(1)}, u32[]{:S(2)}, u32[]{:S(2)}) %all-to-all-start) | async-done | bytes 1048608 | tf_op jit(solution)/shard_map/all_to_all | solution.py:378
  40.0 1.0 copy-done.1
  41.0 4.8 %all-to-all-start.1 = ((bf16[96,136,128]{2,1,0:T(8,128)(2,1)}), bf16[96,136,128]{2,1,0:T(8,128)(2,1)}, u32[]{:S(2)}, u32[]{:S(2)}) async-start(bf16[96,136,128]{2,1,0:T(8,128)(2,1)} %gather_fusion), calls=%async_computation.1 | async-start | bytes 6684672 | tf_op jit(solution)/shard_map/all_to_all | solution.py:394
  45.8 0.9 collective-permute-start.1
  46.7 1.9 %collective-permute-start = (f32[3,4]{1,0:T(4,128)S(1)}, f32[3,4]{1,0:T(4,128)S(1)}, u32[]{:S(2)}, u32[]{:S(2)}) collective-permute-start(f32[3,4]{1,0:T(4,128)S(1)} %copy-done.5), channel_id=1, source_target_pairs={{0,3},{1,0},{2,1},{3,2},{4,7},{5,4},{6,5},{7,6},{8,11},{9,8},{10,9... | collective-permute-start | bytes 152 | tf_op jit(solution)/shard_map/ppermute | solution.py:383
  48.7 1.2 collective-permute-done.1
  49.8 2.8 %collective-permute-done.2 = f32[3,4]{1,0:T(4,128)S(1)} collective-permute-done((f32[3,4]{1,0:T(4,128)S(1)}, f32[3,4]{1,0:T(4,128)S(1)}, u32[]{:S(2)}, u32[]{:S(2)}) %collective-permute-start.2) | collective-permute-done | bytes 80 | tf_op jit(solution)/shard_map/ppermute | solution.py:383
  52.8 22.4 %element_sums.1 = (f32[2048,128]{1,0:T(8,128)}, bf16[4096,128]{1,0:T(8,128)(2,1)}) custom-call(s32[6,1024]{1,0:T(8,128)} %conn_ref.1, bf16[2048,128]{1,0:T(8,128)(2,1)} %x_ref.3, bf16[4096,128]{1,0:T(8,128)(2,1)} %bitcast.23, f32[1024,36]{1,0:T(8,128)} %select_bitcast_fusion.mats_ref), custom_call_target="tpu_custom_call" | custom-call | bytes 67108864 | tf_op jit(solution)/shard_map/element_sums/pallas_call | solution.py:140
  75.2 12.0 %all-to-all-done.1.blocks_ref = bf16[96,136,128]{2,1,0:T(8,128)(2,1)} async-done(((bf16[96,136,128]{2,1,0:T(8,128)(2,1)}), bf16[96,136,128]{2,1,0:T(8,128)(2,1)}, u32[]{:S(2)}, u32[]{:S(2)}) %all-to-all-start.1) | async-done | bytes 3342368 | tf_op jit(solution)/shard_map/all_to_all | solution.py:394
  87.2 6.5 %all-to-all-start.2 = ((bf16[128,32,128]{2,1,0:T(8,128)(2,1)}), bf16[128,32,128]{2,1,0:T(8,128)(2,1)S(1)}, u32[]{:S(2)}, u32[]{:S(2)}) async-start(bf16[128,32,128]{2,1,0:T(8,128)(2,1)} %bitcast.25), calls=%async_computation.2 | async-start | bytes 2097152 | tf_op jit(solution)/shard_map/all_to_all | solution.py:399
  93.7 0.7 broadcast_in_dim.29.waves_ref
  94.3 29.3 %parent_sums.1 = (f32[2,4,2,64,128]{4,3,2,1,0:T(8,128)}, bf16[2,4,2,64,128]{4,3,2,1,0:T(8,128)(2,1)}, bf16[2,4,2,64,128]{4,3,2,1,0:T(8,128)(2,1)}, bf16[2,4,2,64,128]{4,3,2,1,0:T(8,128)(2,1)}) custom-call(bf16[96,136,128]{2,1,0:T(8,128)(2,1)} %all-to-all-done.1.blocks_ref, f32[3,16,128]{2,1,0:T(8,128)} %broadcast_in_dim.29.waves_ref), custom_call_target="tpu_custom_call" | custom-call | flops 12884901888 | bytes 16777216 | tf_op jit(solution)/shard_map/parent_sums/pallas_call | solution.py:317
  123.7 1.4 collective-permute-start.3
  125.1 2.5 %collective-permute-start.4 = (bf16[2,4,2,64,128]{4,3,2,1,0:T(8,128)(2,1)}, bf16[2,4,2,64,128]{4,3,2,1,0:T(8,128)(2,1)S(1)}, u32[]{:S(2)}, u32[]{:S(2)}) collective-permute-start(bf16[2,4,2,64,128]{4,3,2,1,0:T(8,128)(2,1)} %get-tuple-element.24), channel_id=1, source_target_pairs={{0,2},{1,3},{2,0},{3,1},{4,6},{5,7},{6,4},{7,5},{8,10},{9,11},{10,... | collective-permute-start | bytes 786440 | tf_op jit(solution)/shard_map/ppermute | solution.py:409
  127.6 1.1 collective-permute-start.5
  128.7 3.2 %collective-permute-done.3 = bf16[2,4,2,64,128]{4,3,2,1,0:T(8,128)(2,1)S(1)} collective-permute-done((bf16[2,4,2,64,128]{4,3,2,1,0:T(8,128)(2,1)}, bf16[2,4,2,64,128]{4,3,2,1,0:T(8,128)(2,1)S(1)}, u32[]{:S(2)}, u32[]{:S(2)}) %collective-permute-start.3) | collective-permute-done | bytes 262176 | tf_op jit(solution)/shard_map/ppermute | solution.py:409
  131.9 7.6 %collective-permute-done.4 = bf16[2,4,2,64,128]{4,3,2,1,0:T(8,128)(2,1)S(1)} collective-permute-done((bf16[2,4,2,64,128]{4,3,2,1,0:T(8,128)(2,1)}, bf16[2,4,2,64,128]{4,3,2,1,0:T(8,128)(2,1)S(1)}, u32[]{:S(2)}, u32[]{:S(2)}) %collective-permute-start.4) | collective-permute-done | bytes 262176 | tf_op jit(solution)/shard_map/ppermute | solution.py:409
  139.4 2.0 %convert_add_fusion = f32[2,4,2,64,128]{4,3,2,1,0:T(8,128)} fusion(bf16[2,4,2,64,128]{4,3,2,1,0:T(8,128)(2,1)S(1)} %collective-permute-done.5, bf16[2,4,2,64,128]{4,3,2,1,0:T(8,128)(2,1)S(1)} %collective-permute-done.4, f32[2,4,2,64,128]{4,3,2,1,0:T(8,128)} %get-tuple-element.22, bf16[2,4,2,64,128]{4,3,2,1,0:T(8,128)(2,1)S(1)} %collective-permute-done.3), kind=kLoop, calls=%fused_computation.7 | loop fusion | flops 786432 | bytes 1835008 | tf_op jit(solution)/shard_map/add | solution.py:410
  141.4 1.0 copy-done
  142.4 8.1 %fold_back.1 = f32[2048,128]{1,0:T(8,128)} custom-call(s32[1,4096]{1,0:T(1,128)} %reshape.106.list_ref, bf16[4096,128]{1,0:T(8,128)(2,1)} %bitcast.22, f32[2048,128]{1,0:T(8,128)} %get-tuple-element.20.local_ref), custom_call_target="tpu_custom_call" | custom-call | bytes 16777216 | tf_op jit(solution)/shard_map/fold_back/pallas_call | solution.py:178
  (31 shorter events, 0.2 us)
Async XLA Ops:
  0.6 20.0 %copy-start.7 = (s32[32]{0:T(128)S(1)}, s32[32]{0:T(128)}, u32[]{:S(2)}) copy-start(s32[32]{0:T(128)} %param.18) | copy-start | bytes 388
  0.6 20.0 %copy-start.8 = (s32[32]{0:T(128)S(1)}, s32[32]{0:T(128)}, u32[]{:S(2)}) copy-start(s32[32]{0:T(128)} %param.19) | copy-start | bytes 388
  0.7 20.2 %copy-start.6 = (s32[32]{0:T(128)S(1)}, s32[32]{0:T(128)}, u32[]{:S(2)}) copy-start(s32[32]{0:T(128)} %param.20) | copy-start | bytes 388
  0.7 21.7 %copy-start.4 = (bf16[32,3,128]{2,0,1:T(8,128)(2,1)S(1)}, bf16[32,3,128]{2,0,1:T(8,128)(2,1)}, u32[]{:S(2)}) copy-start(bf16[32,3,128]{2,0,1:T(8,128)(2,1)} %param.17) | copy-start | bytes 73732
  0.7 21.7 %copy-start.3 = (f32[36,1024]{1,0:T(8,128)S(1)}, f32[36,1024]{1,0:T(8,128)}, u32[]{:S(2)}) copy-start(f32[36,1024]{1,0:T(8,128)} %param.14) | copy-start | bytes 442372
  2.2 18.7 %copy-start.2 = (s32[128,32]{1,0:T(8,128)S(1)}, s32[128,32]{1,0:T(8,128)}, u32[]{:S(2)}) copy-start(s32[128,32]{1,0:T(8,128)} %copy.23.list_ref) | copy-start | bytes 49156
  9.1 30.9 %all-to-all-start = ((bf16[128,32,128]{2,1,0:T(8,128)(2,1)}), bf16[128,32,128]{2,1,0:T(8,128)(2,1)S(1)}, u32[]{:S(2)}, u32[]{:S(2)}) async-start(bf16[128,32,128]{2,1,0:T(8,128)(2,1)} %bitcast.24), calls=%async_computation | async-start | bytes 2097152 | tf_op jit(solution)/shard_map/all_to_all | solution.py:378
  28.1 17.8 %copy-start.5 = (f32[3,4]{1,0:T(4,128)S(1)}, f32[3,4]{1,0:T(4,128)}, u32[]{:S(2)}) copy-start(f32[3,4]{1,0:T(4,128)} %param.21) | copy-start | bytes 148
  40.0 1.0 copy-start.1
  41.0 46.2 %all-to-all-start.1 = ((bf16[96,136,128]{2,1,0:T(8,128)(2,1)}), bf16[96,136,128]{2,1,0:T(8,128)(2,1)}, u32[]{:S(2)}, u32[]{:S(2)}) async-start(bf16[96,136,128]{2,1,0:T(8,128)(2,1)} %gather_fusion), calls=%async_computation.1 | async-start | bytes 6684672 | tf_op jit(solution)/shard_map/all_to_all | solution.py:394
  45.8 4.0 %collective-permute-start.1 = (f32[3,4]{1,0:T(4,128)S(1)}, f32[3,4]{1,0:T(4,128)S(1)}, u32[]{:S(2)}, u32[]{:S(2)}) collective-permute-start(f32[3,4]{1,0:T(4,128)S(1)} %copy-done.5), channel_id=1, source_target_pairs={{0,2},{1,3},{2,0},{3,1},{4,6},{5,7},{6,4},{7,5},{8,10},{9,11},{10,... | collective-permute-start | bytes 152 | tf_op jit(solution)/shard_map/ppermute | solution.py:383
  46.7 3.1 %collective-permute-start = (f32[3,4]{1,0:T(4,128)S(1)}, f32[3,4]{1,0:T(4,128)S(1)}, u32[]{:S(2)}, u32[]{:S(2)}) collective-permute-start(f32[3,4]{1,0:T(4,128)S(1)} %copy-done.5), channel_id=1, source_target_pairs={{0,3},{1,0},{2,1},{3,2},{4,7},{5,4},{6,5},{7,6},{8,11},{9,8},{10,9... | collective-permute-start | bytes 152 | tf_op jit(solution)/shard_map/ppermute | solution.py:383
  48.6 4.0 %collective-permute-start.2 = (f32[3,4]{1,0:T(4,128)S(1)}, f32[3,4]{1,0:T(4,128)S(1)}, u32[]{:S(2)}, u32[]{:S(2)}) collective-permute-start(f32[3,4]{1,0:T(4,128)S(1)} %copy-done.5), channel_id=1, source_target_pairs={{0,1},{1,2},{2,3},{3,0},{4,5},{5,6},{6,7},{7,4},{8,9},{9,10},{10,1... | collective-permute-start | bytes 152 | tf_op jit(solution)/shard_map/ppermute | solution.py:383
  87.2 54.2 %all-to-all-start.2 = ((bf16[128,32,128]{2,1,0:T(8,128)(2,1)}), bf16[128,32,128]{2,1,0:T(8,128)(2,1)S(1)}, u32[]{:S(2)}, u32[]{:S(2)}) async-start(bf16[128,32,128]{2,1,0:T(8,128)(2,1)} %bitcast.25), calls=%async_computation.2 | async-start | bytes 2097152 | tf_op jit(solution)/shard_map/all_to_all | solution.py:399
  123.7 8.2 %collective-permute-start.3 = (bf16[2,4,2,64,128]{4,3,2,1,0:T(8,128)(2,1)}, bf16[2,4,2,64,128]{4,3,2,1,0:T(8,128)(2,1)S(1)}, u32[]{:S(2)}, u32[]{:S(2)}) collective-permute-start(bf16[2,4,2,64,128]{4,3,2,1,0:T(8,128)(2,1)} %get-tuple-element.23), channel_id=1, source_target_pairs={{0,1},{1,2},{2,3},{3,0},{4,5},{5,6},{6,7},{7,4},{8,9},{9,10},{10,1... | collective-permute-start | bytes 786440 | tf_op jit(solution)/shard_map/ppermute | solution.py:409
  125.1 14.3 %collective-permute-start.4 = (bf16[2,4,2,64,128]{4,3,2,1,0:T(8,128)(2,1)}, bf16[2,4,2,64,128]{4,3,2,1,0:T(8,128)(2,1)S(1)}, u32[]{:S(2)}, u32[]{:S(2)}) collective-permute-start(bf16[2,4,2,64,128]{4,3,2,1,0:T(8,128)(2,1)} %get-tuple-element.24), channel_id=1, source_target_pairs={{0,2},{1,3},{2,0},{3,1},{4,6},{5,7},{6,4},{7,5},{8,10},{9,11},{10,... | collective-permute-start | bytes 786440 | tf_op jit(solution)/shard_map/ppermute | solution.py:409
  127.6 11.8 %collective-permute-start.5 = (bf16[2,4,2,64,128]{4,3,2,1,0:T(8,128)(2,1)}, bf16[2,4,2,64,128]{4,3,2,1,0:T(8,128)(2,1)S(1)}, u32[]{:S(2)}, u32[]{:S(2)}) collective-permute-start(bf16[2,4,2,64,128]{4,3,2,1,0:T(8,128)(2,1)} %get-tuple-element.25), channel_id=1, source_target_pairs={{0,3},{1,0},{2,1},{3,2},{4,7},{5,4},{6,5},{7,6},{8,11},{9,8},{10,9... | collective-permute-start | bytes 786440 | tf_op jit(solution)/shard_map/ppermute | solution.py:409
  141.4 1.0 copy-start

commit v2 on v1

--- a/solution.py
+++ b/solution.py
@@ -28,37 +28,36 @@
     return pltpu.CompilerParams(vmem_limit_bytes=VMEM_LIMIT)
 
 
-def pick_kernel(list_ref, x_ref, out_ref, wide, picked):
+def pick_kernel(list_ref, x_ref, out_ref, flipped):
     owned, columns = x_ref.shape
-    count, width = list_ref.shape
-    wide[0:owned, :] = x_ref[...].astype(jnp.float32)
-    wide[owned : owned + 8, :] = jnp.zeros((8, columns), jnp.float32)
-
-    def one(row, carry):
-        for slot in range(width):
-            picked[pl.ds(row * width + slot, 1), :] = wide[pl.ds(list_ref[row, slot], 1), :]
-        return carry
-
-    lax.fori_loop(0, count, one, 0)
-    out_ref[...] = picked[...].astype(out_ref.dtype)
-
-
-def pick_rows(send_list, x_edges):
+    total = list_ref.shape[1]
+    tile = min(1024, total)
+    flipped[...] = x_ref[...].T
+
+    def one(step, carry):
+        at = pl.ds(pl.multiple_of(step * tile, tile), tile)
+        rows = lax.broadcasted_iota(jnp.int32, (owned, tile), 0)
+        hot = jnp.where(rows == list_ref[:, at], 1.0, 0.0).astype(flipped.dtype)
+        picked = jnp.dot(flipped[...], hot, preferred_element_type=jnp.float32)
+        out_ref[at, :] = picked.T.astype(out_ref.dtype)
+        return carry
+
+    lax.fori_loop(0, total // tile, one, 0)
+
+
+def pick_rows(list_row, x_edges):
     owned, columns = x_edges.shape
-    total = send_list.shape[0] * send_list.shape[1]
+    total = list_row.shape[1]
     return pl.pallas_call(
         pick_kernel,
         out_shape=jax.ShapeDtypeStruct((total, columns), x_edges.dtype),
-        in_specs=[smem(), vmem()],
+        in_specs=[vmem(), vmem()],
         out_specs=vmem(),
-        scratch_shapes=[
-            pltpu.VMEM((owned + 8, columns), jnp.float32),
-            pltpu.VMEM((total, columns), jnp.float32),
-        ],
+        scratch_shapes=[pltpu.VMEM((columns, owned), x_edges.dtype)],
         compiler_params=params(),
         cost_estimate=pl.CostEstimate(flops=0, bytes_accessed=1 << 24, transcendentals=0),
         name="pick_rows",
-    )(send_list, x_edges)
+    )(list_row, x_edges)
 
 
 GROUP = 8
@@ -157,33 +156,41 @@
     )(connectivity, x_edges, halo, mats)
 
 
-def fold_kernel(list_ref, returned_ref, local_ref, out_ref):
-    owned = local_ref.shape[0]
-    total = returned_ref.shape[0]
-    tile = 256
+def fold_kernel(list_ref, returned_ref, local_ref, out_ref, flipped):
+    owned, columns = local_ref.shape
+    tile = FOLD_TILE
+    flipped[...] = returned_ref[...].T
+    lanes = lax.broadcasted_iota(jnp.int32, list_ref.shape, 1)
 
     def one(step, carry):
+        hots = []
+        for part in range(tile // columns):
+            want = lanes + (step * tile + part * columns)
+            hots.append(jnp.where(list_ref[...] == want, 1.0, 0.0).astype(flipped.dtype))
+        total = jnp.dot(
+            flipped[...], jnp.concatenate(hots, axis=1), preferred_element_type=jnp.float32
+        )
         at = pl.ds(pl.multiple_of(step * tile, tile), tile)
-        rows = lax.broadcasted_iota(jnp.int32, (tile, total), 0) + step * tile
-        hot = jnp.where(rows == list_ref[...], 1.0, 0.0).astype(jnp.bfloat16)
-        out_ref[at, :] = local_ref[at, :] + jnp.dot(
-            hot, returned_ref[...], preferred_element_type=jnp.float32
-        )
+        out_ref[at, :] = local_ref[at, :] + total.T
         return carry
 
     lax.fori_loop(0, owned // tile, one, 0)
 
 
-def fold_back(list_row, returned, local):
+FOLD_TILE = 512
+
+
+def fold_back(list_lanes, returned, local):
     return pl.pallas_call(
         fold_kernel,
         out_shape=jax.ShapeDtypeStruct(local.shape, jnp.float32),
         in_specs=[vmem(), vmem(), vmem()],
         out_specs=vmem(),
+        scratch_shapes=[pltpu.VMEM(returned.shape[::-1], returned.dtype)],
         compiler_params=params(),
-        cost_estimate=pl.CostEstimate(flops=0, bytes_accessed=1 << 24, transcendentals=0),
+        cost_estimate=pl.CostEstimate(flops=1 << 32, bytes_accessed=1 << 24, transcendentals=0),
         name="fold_back",
-    )(list_row, returned, local)
+    )(list_lanes, returned, local)
 
 
 def sin_cos_turns(turns):
@@ -202,60 +209,62 @@
     return 2.0 * sine * cosine, 1.0 - 2.0 * sine * sine
 
 
-def digit_polynomial(coords, digit):
-    total = None
+def node_polynomials(coords):
+    away = [coords - t for t in NODE_T]
+    low, high = away[0] * away[1], away[2] * away[3]
+    pairs = [away[1] * high, away[0] * high, low * away[3], low * away[2]]
+    scaled = []
     for j in range(NODES):
-        value = None
-        for i in range(NODES):
-            if i != j:
-                factor = (coords - NODE_T[i]) * (1.0 / (NODE_T[j] - NODE_T[i]))
-                value = factor if value is None else value * factor
-        total = value if total is None else jnp.where(digit == j, value, total)
-    return total
+        scale = math.prod(NODE_T[j] - NODE_T[i] for i in range(NODES) if i != j)
+        scaled.append(pairs[j] * (1.0 / scale))
+    return scaled
 
 
 def parent_kernel(blocks_ref, waves_ref, *refs):
-    outs = refs[:DIRS]
-    weights, sources, sums = refs[DIRS:]
+    outs, (weights, sources, sums) = refs[:-3], refs[-3:]
     slots, unused, columns = blocks_ref.shape
     cones = waves_ref.shape[1]
     size = columns
-    per_dir = cones // DIRS
+    per_dir = cones // len(outs)
     span = sources.shape[0] // size
 
-    lane_rows = lax.broadcasted_iota(jnp.int32, (8, size), 0)
+    sub = lax.broadcasted_iota(jnp.int32, (8, size), 0)
     y_rows = lax.broadcasted_iota(jnp.int32, (size, columns), 0).astype(jnp.float32)
-    third_digit = lane_rows % NODES
-    second_low = lane_rows // NODES
+    y_rows = y_rows.astype(jnp.bfloat16)
+    zero = jnp.zeros((size, columns), jnp.bfloat16)
 
     sums[...] = jnp.zeros_like(sums)
 
     def one(step, carry):
         for part in range(span):
             slot = step * span + part
-            meta = blocks_ref[slot, size : size + 8, :].astype(jnp.float32)
-            block = blocks_ref[slot, 0:size, :].astype(jnp.float32)
-            live = jnp.broadcast_to(meta[7:8, :], (size, columns))
-            parent = jnp.broadcast_to(meta[6:7, :], (size, columns))
-            block = jnp.where(y_rows < live, block, 0.0)
+            tail = blocks_ref[slot, size : size + 8, :]
+            live = jnp.broadcast_to(tail[7:8, :], (size, columns))
+            parent = jnp.broadcast_to(tail[6:7, :], (size, columns))
+            block = jnp.where(y_rows < live, blocks_ref[slot, 0:size, :], zero)
             at = slice(part * size, (part + 1) * size)
-            sources[at, 0:columns] = jnp.where(parent < 0.5, block, 0.0).astype(jnp.bfloat16)
-            sources[at, columns : 2 * columns] = jnp.where(parent > 0.5, block, 0.0).astype(
-                jnp.bfloat16
-            )
+            second_parent = parent > jnp.bfloat16(0.5)
+            sources[at, 0:columns] = jnp.where(second_parent, zero, block)
+            sources[at, columns : 2 * columns] = jnp.where(second_parent, block, zero)
+            meta = tail.astype(jnp.float32)
             shifted = meta[0:3, :] + meta[3:6, :]
             turns = None
             for d in range(3):
                 piece = waves_ref[d] * jnp.broadcast_to(shifted[d : d + 1, :], (cones, size))
                 turns = piece if turns is None else turns + piece
             sine, cosine = sin_cos_turns(turns)
-            coords = shifted * 0.5
-            along = [jnp.broadcast_to(coords[d : d + 1, :], (8, size)) for d in range(3)]
-            third = digit_polynomial(along[2], third_digit)
-            second = [digit_polynomial(along[1], second_low + 2 * h) * third for h in range(2)]
-            first = [
-                digit_polynomial(along[0], jnp.full((8, size), j, jnp.int32)) for j in range(NODES)
+            along = node_polynomials(shifted * 0.5)
+
+            def row(d, j):
+                return jnp.broadcast_to(along[j][d : d + 1, :], (8, size))
+
+            third = row(2, 3)
+            for j in range(NODES - 1):
+                third = jnp.where(sub % NODES == j, row(2, j), third)
+            second = [
+                jnp.where(sub < NODES, row(1, 2 * h), row(1, 2 * h + 1)) * third for h in range(2)
             ]
+            first = [row(0, j) for j in range(NODES)]
             basis = jnp.concatenate([first[v // 2] * second[v % 2] for v in range(8)], axis=0)
             for k in range(cones):
                 base = k * 2 * SQUARE
@@ -265,7 +274,7 @@
                 weights[base + SQUARE : base + 2 * SQUARE, at] = (
                     basis * jnp.broadcast_to(-sine[k : k + 1, :], (SQUARE, size))
                 ).astype(jnp.bfloat16)
-        height = 512
+        height = min(512, cones * 2 * SQUARE)
         for row in range(0, cones * 2 * SQUARE, height):
             sums[row : row + height, :] += jnp.dot(
                 weights[row : row + height, :],
@@ -306,29 +315,28 @@
             out[p, k % per_dir, 1] = (cosine * imag + sine * real).astype(out.dtype)
 
 
-SPAN = 2
-
-
-def parent_sums(blocks, waves):
+SPAN = 8
+
+
+def parent_sums(blocks, waves, dtypes):
     columns = blocks.shape[2]
     cones = waves.shape[1]
-    piece = (2, cones // DIRS, 2, SQUARE, columns)
+    piece = (2, cones // len(dtypes), 2, SQUARE, columns)
     rows = cones * 2 * SQUARE
     return pl.pallas_call(
         parent_kernel,
-        out_shape=(jax.ShapeDtypeStruct(piece, jnp.float32),)
-        + (jax.ShapeDtypeStruct(piece, jnp.bfloat16),) * (DIRS - 1),
+        out_shape=tuple(jax.ShapeDtypeStruct(piece, dtype) for dtype in dtypes),
         in_specs=[vmem(), vmem()],
-        out_specs=(vmem(),) * DIRS,
+        out_specs=(vmem(),) * len(dtypes),
         scratch_shapes=[
-            pltpu.VMEM((rows, SPAN * 128), jnp.bfloat16),
-            pltpu.VMEM((SPAN * 128, 2 * columns), jnp.bfloat16),
+            pltpu.VMEM((rows, SPAN * columns), jnp.bfloat16),
+            pltpu.VMEM((SPAN * columns, 2 * columns), jnp.bfloat16),
             pltpu.VMEM((rows, 2 * columns), jnp.float32),
         ],
         compiler_params=params(),
         cost_estimate=pl.CostEstimate(
-            flops=2 * rows * 2 * columns * blocks.shape[0] * 128,
-            bytes_accessed=1 << 24,
+            flops=2 * rows * 2 * columns * blocks.shape[0] * columns,
+            bytes_accessed=1 << 23,
             transcendentals=0,
         ),
         name="parent_sums",
@@ -374,24 +382,27 @@
     elements = connectivity.shape[1]
     everywhere = ("dom", "dir")
 
-    outgoing = pick_rows(send_list, x_edges).reshape(partitions, width, columns)
+    list_row = send_list.reshape(1, partitions * width)
+    outgoing = pick_rows(list_row, x_edges).reshape(partitions, width, columns)
     halo = lax.all_to_all(outgoing, everywhere, split_axis=0, concat_axis=0, tiled=True)
+
+    list_lanes = jnp.broadcast_to(
+        send_list.reshape(partitions * width, 1), (partitions * width, columns)
+    )
+    live = jnp.arange(elements)[None, :] < elem_live[0]
+    mats = jnp.where(live, elem_mats, 0.0).T
+    currents, list_lanes, mats = lax.optimization_barrier((currents, list_lanes, mats))
+    packed = packed_blocks(currents, positions, block_live, block_owner, block_leaf)
+
+    halo, packed, cone_waves = lax.optimization_barrier((halo, packed, cone_waves))
+    arrived = lax.all_to_all(packed, "dom", split_axis=0, concat_axis=0, tiled=True)
 
     waves = [cone_waves]
     for s in range(1, DIRS):
-        waves.append(
-            lax.ppermute(cone_waves, "dir", [(i, (i - s) % DIRS) for i in range(DIRS)])
-        )
+        waves.append(lax.ppermute(cone_waves, "dir", [(i, (i - s) % DIRS) for i in range(DIRS)]))
     waves = jnp.concatenate(waves, axis=1) * (0.5 / math.pi)
     waves = jnp.broadcast_to(waves[:, :, None], waves.shape + (columns,))
-
-    packed = packed_blocks(currents, positions, block_live, block_owner, block_leaf)
-    live = jnp.arange(elements)[None, :] < elem_live[0]
-    mats = jnp.where(live, elem_mats, 0.0).T
-    list_row = send_list.reshape(1, partitions * width)
-
-    halo, packed, mats, list_row = lax.optimization_barrier((halo, packed, mats, list_row))
-    arrived = lax.all_to_all(packed, "dom", split_axis=0, concat_axis=0, tiled=True)
+    halo, waves = lax.optimization_barrier((halo, waves))
     local, back = element_sums(
         connectivity, x_edges, halo.reshape(partitions * width, columns), mats
     )
@@ -403,12 +414,18 @@
         concat_axis=0,
         tiled=True,
     )
-    pieces = parent_sums(arrived, waves)
+
+    def onward(piece, s):
+        return lax.ppermute(piece, "dir", [(i, (i + s) % DIRS) for i in range(DIRS)])
+
+    half = jnp.bfloat16
+    pieces = parent_sums(arrived, waves, (jnp.float32, half, half, half))
+    moved = [onward(pieces[t], t) for t in range(1, DIRS)]
+    interior_out = fold_back(list_lanes, returned.reshape(partitions * width, columns), local)
+    interior_out, moved = lax.optimization_barrier((interior_out, moved))
     expansions = pieces[0]
-    for s in range(1, DIRS):
-        moved = lax.ppermute(pieces[s], "dir", [(i, (i + s) % DIRS) for i in range(DIRS)])
-        expansions = expansions + moved.astype(jnp.float32)
-    interior_out = fold_back(list_row, returned.reshape(partitions * width, columns), local)
+    for piece in moved:
+        expansions = expansions + piece.astype(jnp.float32)
     return (interior_out, expansions)
 
 

time: 151 us -> 131 us (0.87)
  Pallas kernels: 66.8 us -> 56.5 us
  waiting for transfers between devices: 38.7 us -> 29 us
  local copies, waits for them, and re-layouts: 8.14 us -> 10.6 us
  other arithmetic: 4.74 us -> 2.47 us
    ppermute x3, waiting for transfers between devices: 10.7 us -> 2.98 us  [onward(): lax.ppermute(piece, 'dir', [(i, (i + s) % DIRS) for i in range(DIRS)])]
    pallas_call x1, Pallas kernels: 29.3 us -> 21.9 us  [parent_sums(): pl.pallas_call(parent_kernel, out_shape=tuple((jax.ShapeDtypeStruct(piece...]
    broadcast_in_dim x0 -> x2, local copies, waits for them, and re-layouts: none -> 3.05 us  [shards(): jnp.broadcast_to(send_list.reshape(partitions * width, 1), (partitions *...]
    ppermute x3, waiting for transfers between devices: 4.04 us -> 1.96 us  [shards(): lax.ppermute(cone_waves, 'dir', [(i, (i - s) % DIRS) for i in range(DIRS)])]
    pallas_call x1, Pallas kernels: 6.91 us -> 5.4 us  [pick_rows(): pl.pallas_call(pick_kernel, out_shape=jax.ShapeDtypeStruct((total, column...]
    unnamed x21 -> x23, local copies, waits for them, and re-layouts: 3.69 us -> 3.08 us
  transfers between devices with their start and end apart: 9 -> 9, of which waited for: 6 -> 6; matrix products, arithmetic and copies ran while one was open for 6% -> 7% of each run, Pallas kernels for 34% -> 39%
where the time goes in v2:
time: 131 us
  Pallas kernels  56.5 us (43%)
  starting transfers between devices  30.8 us (24%)
  waiting for transfers between devices  29 us (22%)
  local copies, waits for them, and re-layouts  10.6 us (8%)
  other arithmetic  2.47 us (2%)
  between operations  1.56 us (1%)
    pallas_call x1, Pallas kernels, element_sums(): pl.pallas_call(element_kernel, out_shape=(jax.ShapeDtypeStruct((owned, co...  22.3 us
    pallas_call x1, Pallas kernels, parent_sums(): pl.pallas_call(parent_kernel, out_shape=tuple((jax.ShapeDtypeStruct(piece...  21.9 us
    all_to_all x1, waiting for transfers between devices, shards(): lax.all_to_all(packed, 'dom', split_axis=0, concat_axis=0, tiled=True)  13.3 us
    all_to_all x1, starting transfers between devices, shards(): lax.all_to_all(outgoing, everywhere, split_axis=0, concat_axis=0, tiled=T...  11.5 us
    all_to_all x1, waiting for transfers between devices, shards(): lax.all_to_all(outgoing, everywhere, split_axis=0, concat_axis=0, tiled=T...  10.7 us
    pallas_call x1, Pallas kernels, fold_back(): pl.pallas_call(fold_kernel, out_shape=jax.ShapeDtypeStruct(local.shape, j...  6.8 us
    all_to_all x1, starting transfers between devices, shards(): lax.all_to_all(back.reshape(partitions, width, columns), everywhere, spli...  6.46 us
    pallas_call x1, Pallas kernels, pick_rows(): pl.pallas_call(pick_kernel, out_shape=jax.ShapeDtypeStruct((total, column...  5.4 us
  transfers between devices with their start and end apart: 9, of which 6 were waited for; matrix products, arithmetic and copies ran while one was open for 7% of the time, Pallas kernels for 39%

profile of v2, /device:TPU:1, one launch (start us, length us, event | category | flops | bytes accessed | tf_op | source)
XLA Modules:
  0.0 130.9 jit_solution(6010629745905185452)
XLA Ops:
  0.7 0.9 copy.22
  1.5 0.7 reshape.107.list_ref
  2.2 5.4 %pick_rows.1 = bf16[4096,128]{1,0:T(8,128)(2,1)} custom-call(s32[1,4096]{1,0:T(1,128)} %reshape.107.list_ref, bf16[2048,128]{1,0:T(8,128)(2,1)} %x_ref.3), custom_call_target="tpu_custom_call" | custom-call | bytes 16777216 | tf_op jit(solution)/shard_map/pick_rows/pallas_call | solution.py:51
  7.6 11.5 %all-to-all-start = ((bf16[128,32,128]{2,1,0:T(8,128)(2,1)}), bf16[128,32,128]{2,1,0:T(8,128)(2,1)S(1)}, u32[]{:S(2)}, u32[]{:S(2)}) async-start(bf16[128,32,128]{2,1,0:T(8,128)(2,1)} %bitcast.23), calls=%async_computation | async-start | bytes 2097152 | tf_op jit(solution)/shard_map/all_to_all | solution.py:387
  20.1 0.2 copy.23
  20.3 1.0 select_bitcast_fusion.mats_ref
  21.3 0.1 copy.25
  21.4 3.0 %broadcast_in_dim.29.list_ref = s32[4096,128]{1,0:T(8,128)} broadcast(s32[4096]{0:T(1024)S(1)} %broadcast_in_dim.28), dimensions={0} | broadcast | bytes 2113536 | tf_op jit(solution)/shard_map/broadcast_in_dim | solution.py:389
  24.4 0.2 convert_reduce_fusion
  24.8 0.1 fusion.4
  24.9 2.9 %gather_fusion = bf16[96,136,128]{2,1,0:T(8,128)(2,1)} fusion(bf16[33,136,128]{2,1,0:T(8,128)(2,1)S(1)} %fusion.4, s32[1024]{0:T(1024)S(1)} %pad_clamp_fusion), kind=kCustom, calls=%fused_computation | custom fusion | bytes 6685056 | tf_op jit(solution)/shard_map/gather | solution.py:364
  27.8 10.7 %all-to-all-done = bf16[128,32,128]{2,1,0:T(8,128)(2,1)S(1)} async-done(((bf16[128,32,128]{2,1,0:T(8,128)(2,1)}), bf16[128,32,128]{2,1,0:T(8,128)(2,1)S(1)}, u32[]{:S(2)}, u32[]{:S(2)}) %all-to-all-start) | async-done | bytes 1048608 | tf_op jit(solution)/shard_map/all_to_all | solution.py:387
  38.5 1.0 copy-done
  39.5 4.8 %all-to-all-start.1 = ((bf16[96,136,128]{2,1,0:T(8,128)(2,1)}), bf16[96,136,128]{2,1,0:T(8,128)(2,1)}, u32[]{:S(2)}, u32[]{:S(2)}) async-start(bf16[96,136,128]{2,1,0:T(8,128)(2,1)} %gather_fusion), calls=%async_computation.1 | async-start | bytes 6684672 | tf_op jit(solution)/shard_map/all_to_all | solution.py:398
  44.3 0.4 collective-permute-start.2
  44.8 1.7 %collective-permute-start.1 = (f32[3,4]{1,0:T(4,128)S(1)}, f32[3,4]{1,0:T(4,128)S(1)}, u32[]{:S(2)}, u32[]{:S(2)}) collective-permute-start(f32[3,4]{1,0:T(4,128)S(1)} %copy-done.6), channel_id=1, source_target_pairs={{0,2},{1,3},{2,0},{3,1},{4,6},{5,7},{6,4},{7,5},{8,10},{9,11},{10,... | collective-permute-start | bytes 152 | tf_op jit(solution)/shard_map/ppermute | solution.py:402
  46.4 0.9 collective-permute-start
  47.3 0.7 collective-permute-done.2
  48.1 0.6 collective-permute-done.1
  48.7 0.6 collective-permute-done
  49.4 0.7 broadcast_in_dim.62.waves_ref
  50.0 22.3 %element_sums.1 = (f32[2048,128]{1,0:T(8,128)}, bf16[4096,128]{1,0:T(8,128)(2,1)}) custom-call(s32[6,1024]{1,0:T(8,128)} %conn_ref.1, bf16[2048,128]{1,0:T(8,128)(2,1)} %x_ref.3, bf16[4096,128]{1,0:T(8,128)(2,1)} %bitcast.22, f32[1024,36]{1,0:T(8,128)} %select_bitcast_fusion.mats_ref), custom_call_target="tpu_custom_call" | custom-call | bytes 67108864 | tf_op jit(solution)/shard_map/element_sums/pallas_call | solution.py:139
  72.4 13.3 %all-to-all-done.1.blocks_ref = bf16[96,136,128]{2,1,0:T(8,128)(2,1)} async-done(((bf16[96,136,128]{2,1,0:T(8,128)(2,1)}), bf16[96,136,128]{2,1,0:T(8,128)(2,1)}, u32[]{:S(2)}, u32[]{:S(2)}) %all-to-all-start.1) | async-done | bytes 3342368 | tf_op jit(solution)/shard_map/all_to_all | solution.py:398
  85.7 6.5 %all-to-all-start.2 = ((bf16[128,32,128]{2,1,0:T(8,128)(2,1)}), bf16[128,32,128]{2,1,0:T(8,128)(2,1)S(1)}, u32[]{:S(2)}, u32[]{:S(2)}) async-start(bf16[128,32,128]{2,1,0:T(8,128)(2,1)} %bitcast.24), calls=%async_computation.2 | async-start | bytes 2097152 | tf_op jit(solution)/shard_map/all_to_all | solution.py:410
  92.2 21.9 %parent_sums.1 = (f32[2,4,2,64,128]{4,3,2,1,0:T(8,128)}, bf16[2,4,2,64,128]{4,3,2,1,0:T(8,128)(2,1)}, bf16[2,4,2,64,128]{4,3,2,1,0:T(8,128)(2,1)}, bf16[2,4,2,64,128]{4,3,2,1,0:T(8,128)(2,1)}) custom-call(bf16[96,136,128]{2,1,0:T(8,128)(2,1)} %all-to-all-done.1.blocks_ref, f32[3,16,128]{2,1,0:T(8,128)} %broadcast_in_dim.62.waves_ref), custom_call_target="tpu_custom_call" | custom-call | flops 12884901888 | bytes 8388608 | tf_op jit(solution)/shard_map/parent_sums/pallas_call | solution.py:326
  114.1 1.4 %collective-permute-start.3 = (bf16[2,4,2,64,128]{4,3,2,1,0:T(8,128)(2,1)}, bf16[2,4,2,64,128]{4,3,2,1,0:T(8,128)(2,1)S(1)}, u32[]{:S(2)}, u32[]{:S(2)}) collective-permute-start(bf16[2,4,2,64,128]{4,3,2,1,0:T(8,128)(2,1)} %get-tuple-element.34), channel_id=1, source_target_pairs={{0,1},{1,2},{2,3},{3,0},{4,5},{5,6},{6,7},{7,4},{8,9},{9,10},{10,1... | collective-permute-start | bytes 786440 | tf_op jit(solution)/shard_map/ppermute | solution.py:419
  115.6 2.5 %collective-permute-start.4 = (bf16[2,4,2,64,128]{4,3,2,1,0:T(8,128)(2,1)}, bf16[2,4,2,64,128]{4,3,2,1,0:T(8,128)(2,1)S(1)}, u32[]{:S(2)}, u32[]{:S(2)}) collective-permute-start(bf16[2,4,2,64,128]{4,3,2,1,0:T(8,128)(2,1)} %get-tuple-element.35), channel_id=1, source_target_pairs={{0,2},{1,3},{2,0},{3,1},{4,6},{5,7},{6,4},{7,5},{8,10},{9,11},{10,... | collective-permute-start | bytes 786440 | tf_op jit(solution)/shard_map/ppermute | solution.py:419
  118.1 1.1 collective-permute-start.5
  119.2 1.0 copy-done.1
  120.2 6.8 %fold_back.1 = f32[2048,128]{1,0:T(8,128)} custom-call(s32[4096,128]{1,0:T(8,128)} %broadcast_in_dim.29.list_ref, bf16[4096,128]{1,0:T(8,128)(2,1)} %bitcast.25, f32[2048,128]{1,0:T(8,128)} %get-tuple-element.31.local_ref), custom_call_target="tpu_custom_call" | custom-call | flops 4294967296 | bytes 16777216 | tf_op jit(solution)/shard_map/fold_back/pallas_call | solution.py:184
  127.0 3.0 %collective-permute-done.4 = bf16[2,4,2,64,128]{4,3,2,1,0:T(8,128)(2,1)S(1)} collective-permute-done((bf16[2,4,2,64,128]{4,3,2,1,0:T(8,128)(2,1)}, bf16[2,4,2,64,128]{4,3,2,1,0:T(8,128)(2,1)S(1)}, u32[]{:S(2)}, u32[]{:S(2)}) %collective-permute-start.4) | collective-permute-done | bytes 262176 | tf_op jit(solution)/shard_map/ppermute | solution.py:419
  130.0 0.9 convert_add_fusion
  (35 shorter events, 0.5 us)
Async XLA Ops:
  0.6 19.3 %copy-start.8 = (s32[32]{0:T(128)S(1)}, s32[32]{0:T(128)}, u32[]{:S(2)}) copy-start(s32[32]{0:T(128)} %param.18) | copy-start | bytes 388
  0.6 19.4 %copy-start.7 = (s32[32]{0:T(128)S(1)}, s32[32]{0:T(128)}, u32[]{:S(2)}) copy-start(s32[32]{0:T(128)} %param.20) | copy-start | bytes 388
  0.7 19.4 %copy-start.4 = (f32[36,1024]{1,0:T(8,128)S(1)}, f32[36,1024]{1,0:T(8,128)}, u32[]{:S(2)}) copy-start(f32[36,1024]{1,0:T(8,128)} %param.14) | copy-start | bytes 442372
  7.6 13.8 %copy-start.5 = (bf16[32,3,128]{2,0,1:T(8,128)(2,1)S(1)}, bf16[32,3,128]{2,0,1:T(8,128)(2,1)}, u32[]{:S(2)}) copy-start(bf16[32,3,128]{2,0,1:T(8,128)(2,1)} %param.17) | copy-start | bytes 73732
  7.6 30.9 %all-to-all-start = ((bf16[128,32,128]{2,1,0:T(8,128)(2,1)}), bf16[128,32,128]{2,1,0:T(8,128)(2,1)S(1)}, u32[]{:S(2)}, u32[]{:S(2)}) async-start(bf16[128,32,128]{2,1,0:T(8,128)(2,1)} %bitcast.23), calls=%async_computation | async-start | bytes 2097152 | tf_op jit(solution)/shard_map/all_to_all | solution.py:387
  19.1 5.3 %copy-start.9 = (s32[32]{0:T(128)S(1)}, s32[32]{0:T(128)}, u32[]{:S(2)}) copy-start(s32[32]{0:T(128)} %param.19) | copy-start | bytes 388
  19.1 5.7 %copy-start.2 = (bf16[32,128,128]{2,1,0:T(8,128)(2,1)S(1)}, bf16[32,128,128]{2,1,0:T(8,128)(2,1)}, u32[]{:S(2)}) copy-start(bf16[32,128,128]{2,1,0:T(8,128)(2,1)} %param.16) | copy-start | bytes 3145732
  27.8 16.5 %copy-start.6 = (f32[3,4]{1,0:T(4,128)S(1)}, f32[3,4]{1,0:T(4,128)}, u32[]{:S(2)}) copy-start(f32[3,4]{1,0:T(4,128)} %param.21) | copy-start | bytes 148
  38.5 1.0 copy-start
  39.5 46.2 %all-to-all-start.1 = ((bf16[96,136,128]{2,1,0:T(8,128)(2,1)}), bf16[96,136,128]{2,1,0:T(8,128)(2,1)}, u32[]{:S(2)}, u32[]{:S(2)}) async-start(bf16[96,136,128]{2,1,0:T(8,128)(2,1)} %gather_fusion), calls=%async_computation.1 | async-start | bytes 6684672 | tf_op jit(solution)/shard_map/all_to_all | solution.py:398
  44.3 3.7 %collective-permute-start.2 = (f32[3,4]{1,0:T(4,128)S(1)}, f32[3,4]{1,0:T(4,128)S(1)}, u32[]{:S(2)}, u32[]{:S(2)}) collective-permute-start(f32[3,4]{1,0:T(4,128)S(1)} %copy-done.6), channel_id=1, source_target_pairs={{0,1},{1,2},{2,3},{3,0},{4,5},{5,6},{6,7},{7,4},{8,9},{9,10},{10,1... | collective-permute-start | bytes 152 | tf_op jit(solution)/shard_map/ppermute | solution.py:402
  44.8 3.9 %collective-permute-start.1 = (f32[3,4]{1,0:T(4,128)S(1)}, f32[3,4]{1,0:T(4,128)S(1)}, u32[]{:S(2)}, u32[]{:S(2)}) collective-permute-start(f32[3,4]{1,0:T(4,128)S(1)} %copy-done.6), channel_id=1, source_target_pairs={{0,2},{1,3},{2,0},{3,1},{4,6},{5,7},{6,4},{7,5},{8,10},{9,11},{10,... | collective-permute-start | bytes 152 | tf_op jit(solution)/shard_map/ppermute | solution.py:402
  46.4 2.8 %collective-permute-start = (f32[3,4]{1,0:T(4,128)S(1)}, f32[3,4]{1,0:T(4,128)S(1)}, u32[]{:S(2)}, u32[]{:S(2)}) collective-permute-start(f32[3,4]{1,0:T(4,128)S(1)} %copy-done.6), channel_id=1, source_target_pairs={{0,3},{1,0},{2,1},{3,2},{4,7},{5,4},{6,5},{7,6},{8,11},{9,8},{10,9... | collective-permute-start | bytes 152 | tf_op jit(solution)/shard_map/ppermute | solution.py:402
  85.7 33.5 %all-to-all-start.2 = ((bf16[128,32,128]{2,1,0:T(8,128)(2,1)}), bf16[128,32,128]{2,1,0:T(8,128)(2,1)S(1)}, u32[]{:S(2)}, u32[]{:S(2)}) async-start(bf16[128,32,128]{2,1,0:T(8,128)(2,1)} %bitcast.24), calls=%async_computation.2 | async-start | bytes 2097152 | tf_op jit(solution)/shard_map/all_to_all | solution.py:410
  114.1 12.9 %collective-permute-start.3 = (bf16[2,4,2,64,128]{4,3,2,1,0:T(8,128)(2,1)}, bf16[2,4,2,64,128]{4,3,2,1,0:T(8,128)(2,1)S(1)}, u32[]{:S(2)}, u32[]{:S(2)}) collective-permute-start(bf16[2,4,2,64,128]{4,3,2,1,0:T(8,128)(2,1)} %get-tuple-element.34), channel_id=1, source_target_pairs={{0,1},{1,2},{2,3},{3,0},{4,5},{5,6},{6,7},{7,4},{8,9},{9,10},{10,1... | collective-permute-start | bytes 786440 | tf_op jit(solution)/shard_map/ppermute | solution.py:419
  115.6 14.4 %collective-permute-start.4 = (bf16[2,4,2,64,128]{4,3,2,1,0:T(8,128)(2,1)}, bf16[2,4,2,64,128]{4,3,2,1,0:T(8,128)(2,1)S(1)}, u32[]{:S(2)}, u32[]{:S(2)}) collective-permute-start(bf16[2,4,2,64,128]{4,3,2,1,0:T(8,128)(2,1)} %get-tuple-element.35), channel_id=1, source_target_pairs={{0,2},{1,3},{2,0},{3,1},{4,6},{5,7},{6,4},{7,5},{8,10},{9,11},{10,... | collective-permute-start | bytes 786440 | tf_op jit(solution)/shard_map/ppermute | solution.py:419
  118.1 11.9 %collective-permute-start.5 = (bf16[2,4,2,64,128]{4,3,2,1,0:T(8,128)(2,1)}, bf16[2,4,2,64,128]{4,3,2,1,0:T(8,128)(2,1)S(1)}, u32[]{:S(2)}, u32[]{:S(2)}) collective-permute-start(bf16[2,4,2,64,128]{4,3,2,1,0:T(8,128)(2,1)} %get-tuple-element.36), channel_id=1, source_target_pairs={{0,3},{1,0},{2,1},{3,2},{4,7},{5,4},{6,5},{7,6},{8,11},{9,8},{10,9... | collective-permute-start | bytes 786440 | tf_op jit(solution)/shard_map/ppermute | solution.py:419
  119.2 1.0 copy-start.1
  120.2 9.8 %copy-start.3 = (f32[2,4,2,64,128]{4,3,2,1,0:T(8,128)S(1)}, f32[2,4,2,64,128]{4,3,2,1,0:T(8,128)}, u32[]{:S(2)}) copy-start(f32[2,4,2,64,128]{4,3,2,1,0:T(8,128)} %get-tuple-element.38) | copy-start | bytes 1572868

commit v3 on v2

--- a/solution.py
+++ b/solution.py
@@ -12,7 +12,6 @@
 SQUARE = NODES**3
 DIRS = 4
 ROWS = 136
-VMEM_LIMIT = 60 * 1024 * 1024
 NODE_T = [math.cos((2 * j + 1) * math.pi / (2 * NODES)) for j in range(NODES)]
 
 
@@ -24,8 +23,8 @@
     return pl.BlockSpec(memory_space=pltpu.SMEM)
 
 
-def params():
-    return pltpu.CompilerParams(vmem_limit_bytes=VMEM_LIMIT)
+def params(mebibytes):
+    return pltpu.CompilerParams(vmem_limit_bytes=mebibytes * 1024 * 1024)
 
 
 def pick_kernel(list_ref, x_ref, out_ref, flipped):
@@ -54,7 +53,7 @@
         in_specs=[vmem(), vmem()],
         out_specs=vmem(),
         scratch_shapes=[pltpu.VMEM((columns, owned), x_edges.dtype)],
-        compiler_params=params(),
+        compiler_params=params(24),
         cost_estimate=pl.CostEstimate(flops=0, bytes_accessed=1 << 24, transcendentals=0),
         name="pick_rows",
     )(list_row, x_edges)
@@ -150,7 +149,7 @@
             pltpu.VMEM((6 * GROUP * PAIR, columns), jnp.float32),
         ]
         + [pltpu.VMEM((owned + slots, columns), jnp.float32) for _ in range(6)],
-        compiler_params=params(),
+        compiler_params=params(40),
         cost_estimate=pl.CostEstimate(flops=0, bytes_accessed=1 << 26, transcendentals=0),
         name="element_sums",
     )(connectivity, x_edges, halo, mats)
@@ -187,7 +186,7 @@
         in_specs=[vmem(), vmem(), vmem()],
         out_specs=vmem(),
         scratch_shapes=[pltpu.VMEM(returned.shape[::-1], returned.dtype)],
-        compiler_params=params(),
+        compiler_params=params(50),
         cost_estimate=pl.CostEstimate(flops=1 << 32, bytes_accessed=1 << 24, transcendentals=0),
         name="fold_back",
     )(list_lanes, returned, local)
@@ -220,13 +219,24 @@
     return scaled
 
 
-def parent_kernel(blocks_ref, waves_ref, *refs):
-    outs, (weights, sources, sums) = refs[:-3], refs[-3:]
+def parent_kernel(arrived_ref, waves_ref, *refs):
+    outs, (blocks_ref, weights_0, sources_0, weights_1, sources_1, sums, landed) = (
+        refs[:-7],
+        refs[-7:],
+    )
     slots, unused, columns = blocks_ref.shape
     cones = waves_ref.shape[1]
     size = columns
     per_dir = cones // len(outs)
-    span = sources.shape[0] // size
+    span = sources_0.shape[0] // size
+    steps = slots // span
+
+    def fetch(step):
+        at = pl.ds(step * span, span)
+        return pltpu.make_async_copy(arrived_ref.at[at], blocks_ref.at[at], landed.at[step])
+
+    for step in range(steps):
+        fetch(step).start()
 
     sub = lax.broadcasted_iota(jnp.int32, (8, size), 0)
     y_rows = lax.broadcasted_iota(jnp.int32, (size, columns), 0).astype(jnp.float32)
@@ -235,55 +245,75 @@
 
     sums[...] = jnp.zeros_like(sums)
 
-    def one(step, carry):
-        for part in range(span):
-            slot = step * span + part
-            tail = blocks_ref[slot, size : size + 8, :]
-            live = jnp.broadcast_to(tail[7:8, :], (size, columns))
-            parent = jnp.broadcast_to(tail[6:7, :], (size, columns))
-            block = jnp.where(y_rows < live, blocks_ref[slot, 0:size, :], zero)
-            at = slice(part * size, (part + 1) * size)
-            second_parent = parent > jnp.bfloat16(0.5)
-            sources[at, 0:columns] = jnp.where(second_parent, zero, block)
-            sources[at, columns : 2 * columns] = jnp.where(second_parent, block, zero)
-            meta = tail.astype(jnp.float32)
-            shifted = meta[0:3, :] + meta[3:6, :]
-            turns = None
-            for d in range(3):
-                piece = waves_ref[d] * jnp.broadcast_to(shifted[d : d + 1, :], (cones, size))
-                turns = piece if turns is None else turns + piece
-            sine, cosine = sin_cos_turns(turns)
-            along = node_polynomials(shifted * 0.5)
-
-            def row(d, j):
-                return jnp.broadcast_to(along[j][d : d + 1, :], (8, size))
-
-            third = row(2, 3)
-            for j in range(NODES - 1):
-                third = jnp.where(sub % NODES == j, row(2, j), third)
-            second = [
-                jnp.where(sub < NODES, row(1, 2 * h), row(1, 2 * h + 1)) * third for h in range(2)
-            ]
-            first = [row(0, j) for j in range(NODES)]
-            basis = jnp.concatenate([first[v // 2] * second[v % 2] for v in range(8)], axis=0)
-            for k in range(cones):
-                base = k * 2 * SQUARE
-                weights[base : base + SQUARE, at] = (
-                    basis * jnp.broadcast_to(cosine[k : k + 1, :], (SQUARE, size))
-                ).astype(jnp.bfloat16)
-                weights[base + SQUARE : base + 2 * SQUARE, at] = (
-                    basis * jnp.broadcast_to(-sine[k : k + 1, :], (SQUARE, size))
-                ).astype(jnp.bfloat16)
-        height = min(512, cones * 2 * SQUARE)
-        for row in range(0, cones * 2 * SQUARE, height):
+    def prepare(step, part, weights, sources):
+        slot = step * span + part
+        tail = blocks_ref[slot, size : size + 8, :]
+        live = jnp.broadcast_to(tail[7:8, :], (size, columns))
+        parent = jnp.broadcast_to(tail[6:7, :], (size, columns))
+        block = jnp.where(y_rows < live, blocks_ref[slot, 0:size, :], zero)
+        at = slice(part * size, (part + 1) * size)
+        second_parent = parent > jnp.bfloat16(0.5)
+        sources[at, 0:columns] = jnp.where(second_parent, zero, block)
+        sources[at, columns : 2 * columns] = jnp.where(second_parent, block, zero)
+        meta = tail.astype(jnp.float32)
+        shifted = meta[0:3, :] + meta[3:6, :]
+        turns = None
+        for d in range(3):
+            piece = waves_ref[d] * jnp.broadcast_to(shifted[d : d + 1, :], (cones, size))
+            turns = piece if turns is None else turns + piece
+        sine, cosine = sin_cos_turns(turns)
+        along = node_polynomials(shifted * 0.5)
+
+        def row(d, j):
+            return jnp.broadcast_to(along[j][d : d + 1, :], (8, size))
+
+        third = row(2, 3)
+        for j in range(NODES - 1):
+            third = jnp.where(sub % NODES == j, row(2, j), third)
+        second = [
+            jnp.where(sub < NODES, row(1, 2 * h), row(1, 2 * h + 1)) * third for h in range(2)
+        ]
+        first = [row(0, j) for j in range(NODES)]
+        basis = jnp.concatenate([first[v // 2] * second[v % 2] for v in range(8)], axis=0)
+        for k in range(cones):
+            base = k * 2 * SQUARE
+            weights[base : base + SQUARE, at] = (
+                basis * jnp.broadcast_to(cosine[k : k + 1, :], (SQUARE, size))
+            ).astype(jnp.bfloat16)
+            weights[base + SQUARE : base + 2 * SQUARE, at] = (
+                basis * jnp.broadcast_to(-sine[k : k + 1, :], (SQUARE, size))
+            ).astype(jnp.bfloat16)
+
+    height = min(512, cones * 2 * SQUARE)
+    chunks = cones * 2 * SQUARE // height
+    share = max(1, span // chunks)
+
+    def work(weights, sources, step, later_weights, later_sources):
+        for chunk in range(chunks):
+            row = chunk * height
             sums[row : row + height, :] += jnp.dot(
-                weights[row : row + height, :],
-                sources[...],
-                preferred_element_type=jnp.float32,
+                weights[row : row + height, :], sources[...], preferred_element_type=jnp.float32
             )
-        return carry
-
-    lax.fori_loop(0, slots // span, one, 0)
+            for part in range(chunk * share, min(span, (chunk + 1) * share)):
+                prepare(step, part, later_weights, later_sources)
+
+    fetch(0).wait()
+    for part in range(span):
+        prepare(0, part, weights_0, sources_0)
+
+    def two(pair, carry):
+        later = jnp.minimum(2 * pair + 2, steps - 1)
+        fetch(2 * pair + 1).wait()
+
+        @pl.when(2 * pair + 2 < steps)
+        def _():
+            fetch(later).wait()
+
+        work(weights_0, sources_0, 2 * pair + 1, weights_1, sources_1)
+        work(weights_1, sources_1, later, weights_0, sources_0)
+        return carry
+
+    lax.fori_loop(0, steps // 2, two, 0)
 
     node_rows = lax.broadcasted_iota(jnp.int32, (SQUARE, columns), 0)
 
@@ -326,14 +356,18 @@
     return pl.pallas_call(
         parent_kernel,
         out_shape=tuple(jax.ShapeDtypeStruct(piece, dtype) for dtype in dtypes),
-        in_specs=[vmem(), vmem()],
+        in_specs=[pl.BlockSpec(memory_space=pl.ANY), vmem()],
         out_specs=(vmem(),) * len(dtypes),
         scratch_shapes=[
+            pltpu.VMEM(blocks.shape, blocks.dtype),
+            pltpu.VMEM((rows, SPAN * columns), jnp.bfloat16),
+            pltpu.VMEM((SPAN * columns, 2 * columns), jnp.bfloat16),
             pltpu.VMEM((rows, SPAN * columns), jnp.bfloat16),
             pltpu.VMEM((SPAN * columns, 2 * columns), jnp.bfloat16),
             pltpu.VMEM((rows, 2 * columns), jnp.float32),
+            pltpu.SemaphoreType.DMA((blocks.shape[0] // SPAN,)),
         ],
-        compiler_params=params(),
+        compiler_params=params(60),
         cost_estimate=pl.CostEstimate(
             flops=2 * rows * 2 * columns * blocks.shape[0] * columns,
             bytes_accessed=1 << 23,

time: 131 us -> 129 us (0.985)
  Pallas kernels: 56.5 us -> 53 us
  waiting for transfers between devices: 29 us -> 30.8 us
  local copies, waits for them, and re-layouts: 10.6 us -> 9.07 us
    ppermute x3, waiting for transfers between devices: 2.98 us -> 4.56 us  [onward(): lax.ppermute(piece, 'dir', [(i, (i + s) % DIRS) for i in range(DIRS)])]
  transfers between devices with their start and end apart: 9 -> 9, of which waited for: 6 -> 6; matrix products, arithmetic and copies ran while one was open for 7% -> 7% of each run, Pallas kernels for 39% -> 38%
where the time goes in v3:
time: 129 us; the launch traced here: 128 us
  Pallas kernels  53 us (41%)
  starting transfers between devices  30.9 us (24%)
  waiting for transfers between devices  30.8 us (24%)
  local copies, waits for them, and re-layouts  9.07 us (7%)
  other arithmetic  2.9 us (2%)
  between operations  1.49 us (1%)
    pallas_call x1, Pallas kernels, element_sums(): pl.pallas_call(element_kernel, out_shape=(jax.ShapeDtypeStruct((owned, co...  21.7 us
    pallas_call x1, Pallas kernels, parent_sums(): pl.pallas_call(parent_kernel, out_shape=tuple((jax.ShapeDtypeStruct(piece...  20.7 us
    all_to_all x1, waiting for transfers between devices, shards(): lax.all_to_all(packed, 'dom', split_axis=0, concat_axis=0, tiled=True)  14 us
    all_to_all x1, starting transfers between devices, shards(): lax.all_to_all(outgoing, everywhere, split_axis=0, concat_axis=0, tiled=T...  11.5 us
    all_to_all x1, waiting for transfers between devices, shards(): lax.all_to_all(outgoing, everywhere, split_axis=0, concat_axis=0, tiled=T...  10.4 us
    all_to_all x1, starting transfers between devices, shards(): lax.all_to_all(back.reshape(partitions, width, columns), everywhere, spli...  6.47 us
    pallas_call x1, Pallas kernels, fold_back(): pl.pallas_call(fold_kernel, out_shape=jax.ShapeDtypeStruct(local.shape, j...  6.22 us
    ppermute x3, starting transfers between devices, onward(): lax.ppermute(piece, 'dir', [(i, (i + s) % DIRS) for i in range(DIRS)])  5.16 us
  transfers between devices with their start and end apart: 9, of which 6 were waited for; matrix products, arithmetic and copies ran while one was open for 7% of the time, Pallas kernels for 38%

profile of v3, /device:TPU:1, one launch (start us, length us, event | category | flops | bytes accessed | tf_op | source)
XLA Modules:
  0.0 128.2 jit_solution(11716322995110903148)
XLA Ops:
  0.6 0.9 copy.22
  1.5 0.1 reshape.107.list_ref
  1.6 1.0 copy-done
  2.6 4.3 %pick_rows.1 = bf16[4096,128]{1,0:T(8,128)(2,1)} custom-call(s32[1,4096]{1,0:T(1,128)S(1)} %reshape.107.list_ref, bf16[2048,128]{1,0:T(8,128)(2,1)S(1)} %copy-done), custom_call_target="tpu_custom_call" | custom-call | bytes 16777216 | tf_op jit(solution)/shard_map/pick_rows/pallas_call | solution.py:50
  7.0 11.5 %all-to-all-start = ((bf16[128,32,128]{2,1,0:T(8,128)(2,1)}), bf16[128,32,128]{2,1,0:T(8,128)(2,1)S(1)}, u32[]{:S(2)}, u32[]{:S(2)}) async-start(bf16[128,32,128]{2,1,0:T(8,128)(2,1)} %bitcast.2), calls=%async_computation | async-start | bytes 2097152 | tf_op jit(solution)/shard_map/all_to_all | solution.py:421
  19.3 0.2 copy.23
  19.6 0.2 select_bitcast_fusion.mats_ref
  19.8 0.1 copy.25
  19.9 3.0 %broadcast_in_dim.29.list_ref = s32[4096,128]{1,0:T(8,128)} broadcast(s32[4096]{0:T(1024)S(1)} %broadcast_in_dim.28), dimensions={0} | broadcast | bytes 2113536 | tf_op jit(solution)/shard_map/broadcast_in_dim | solution.py:423
  22.9 0.2 convert_reduce_fusion
  23.2 0.1 broadcast_in_dim.36
  23.3 1.3 %fusion.4 = bf16[33,136,128]{2,1,0:T(8,128)(2,1)S(1)} fusion(bf16[32,5,128]{2,1,0:T(8,128)(2,1)S(1)} %broadcast_in_dim.36, bf16[32,3,128]{2,1,0:T(4,128)(2,1)S(1)} %copy.26, bf16[32,128,128]{2,1,0:T(8,128)(2,1)} %param.16), kind=kLoop, calls=%fused_computation.6 | loop fusion | flops 5744640 | bytes 2263040 | tf_op jit(solution)/shard_map/concatenate | solution.py:389
  24.7 2.9 %gather_fusion = bf16[96,136,128]{2,1,0:T(8,128)(2,1)} fusion(bf16[33,136,128]{2,1,0:T(8,128)(2,1)S(1)} %fusion.4, s32[1024]{0:T(1024)S(1)} %pad_clamp_fusion), kind=kCustom, calls=%fused_computation | custom fusion | bytes 6685056 | tf_op jit(solution)/shard_map/gather | solution.py:398
  27.5 10.4 %all-to-all-done = bf16[128,32,128]{2,1,0:T(8,128)(2,1)S(1)} async-done(((bf16[128,32,128]{2,1,0:T(8,128)(2,1)}), bf16[128,32,128]{2,1,0:T(8,128)(2,1)S(1)}, u32[]{:S(2)}, u32[]{:S(2)}) %all-to-all-start) | async-done | bytes 1048608 | tf_op jit(solution)/shard_map/all_to_all | solution.py:421
  37.9 4.8 %all-to-all-start.1 = ((bf16[96,136,128]{2,1,0:T(8,128)(2,1)}), bf16[96,136,128]{2,1,0:T(8,128)(2,1)}, u32[]{:S(2)}, u32[]{:S(2)}) async-start(bf16[96,136,128]{2,1,0:T(8,128)(2,1)} %gather_fusion), calls=%async_computation.1 | async-start | bytes 6684672 | tf_op jit(solution)/shard_map/all_to_all | solution.py:432
  42.7 0.4 collective-permute-start.2
  43.2 1.7 %collective-permute-start.1 = (f32[3,4]{1,0:T(4,128)S(1)}, f32[3,4]{1,0:T(4,128)S(1)}, u32[]{:S(2)}, u32[]{:S(2)}) collective-permute-start(f32[3,4]{1,0:T(4,128)S(1)} %copy-done.6), channel_id=1, source_target_pairs={{0,2},{1,3},{2,0},{3,1},{4,6},{5,7},{6,4},{7,5},{8,10},{9,11},{10,... | collective-permute-start | bytes 152 | tf_op jit(solution)/shard_map/ppermute | solution.py:436
  44.8 0.9 collective-permute-start
  45.7 0.7 collective-permute-done.2
  46.5 0.6 collective-permute-done.1
  47.1 0.6 collective-permute-done
  47.8 0.7 broadcast_in_dim.62.waves_ref
  48.4 21.7 %element_sums.1 = (f32[2048,128]{1,0:T(8,128)S(1)}, bf16[4096,128]{1,0:T(8,128)(2,1)}) custom-call(s32[6,1024]{1,0:T(8,128)S(1)} %copy-done.2, bf16[2048,128]{1,0:T(8,128)(2,1)S(1)} %copy-done.1, bf16[4096,128]{1,0:T(8,128)(2,1)S(1)} %bitcast.22, f32[1024,36]{1,0:T(8,128)S(1)} %select_bitcast_fusion.mats_ref), custom_call_target="tpu_custom_call" | custom-call | bytes 67108864 | tf_op jit(solution)/shard_map/element_sums/pallas_call | solution.py:138
  70.2 14.0 %all-to-all-done.1.arrived_ref = bf16[96,136,128]{2,1,0:T(8,128)(2,1)} async-done(((bf16[96,136,128]{2,1,0:T(8,128)(2,1)}), bf16[96,136,128]{2,1,0:T(8,128)(2,1)}, u32[]{:S(2)}, u32[]{:S(2)}) %all-to-all-start.1) | async-done | bytes 3342368 | tf_op jit(solution)/shard_map/all_to_all | solution.py:432
  84.1 6.5 %all-to-all-start.2 = ((bf16[128,32,128]{2,1,0:T(8,128)(2,1)}), bf16[128,32,128]{2,1,0:T(8,128)(2,1)S(1)}, u32[]{:S(2)}, u32[]{:S(2)}) async-start(bf16[128,32,128]{2,1,0:T(8,128)(2,1)} %bitcast.11), calls=%async_computation.2 | async-start | bytes 2097152 | tf_op jit(solution)/shard_map/all_to_all | solution.py:444
  90.6 20.7 %parent_sums.1 = (f32[2,4,2,64,128]{4,3,2,1,0:T(8,128)}, bf16[2,4,2,64,128]{4,3,2,1,0:T(8,128)(2,1)}, bf16[2,4,2,64,128]{4,3,2,1,0:T(8,128)(2,1)}, bf16[2,4,2,64,128]{4,3,2,1,0:T(8,128)(2,1)}) custom-call(bf16[96,136,128]{2,1,0:T(8,128)(2,1)} %all-to-all-done.1.arrived_ref, f32[3,16,128]{2,1,0:T(8,128)} %broadcast_in_dim.62.waves_ref), custom_call_target="tpu_custom_call" | custom-call | flops 12884901888 | bytes 8388608 | tf_op jit(solution)/shard_map/parent_sums/pallas_call | solution.py:356
  111.3 1.5 %collective-permute-start.3 = (bf16[2,4,2,64,128]{4,3,2,1,0:T(8,128)(2,1)}, bf16[2,4,2,64,128]{4,3,2,1,0:T(8,128)(2,1)S(1)}, u32[]{:S(2)}, u32[]{:S(2)}) collective-permute-start(bf16[2,4,2,64,128]{4,3,2,1,0:T(8,128)(2,1)} %get-tuple-element.34), channel_id=1, source_target_pairs={{0,1},{1,2},{2,3},{3,0},{4,5},{5,6},{6,7},{7,4},{8,9},{9,10},{10,1... | collective-permute-start | bytes 786440 | tf_op jit(solution)/shard_map/ppermute | solution.py:453
  112.8 2.5 %collective-permute-start.4 = (bf16[2,4,2,64,128]{4,3,2,1,0:T(8,128)(2,1)}, bf16[2,4,2,64,128]{4,3,2,1,0:T(8,128)(2,1)S(1)}, u32[]{:S(2)}, u32[]{:S(2)}) collective-permute-start(bf16[2,4,2,64,128]{4,3,2,1,0:T(8,128)(2,1)} %get-tuple-element.35), channel_id=1, source_target_pairs={{0,2},{1,3},{2,0},{3,1},{4,6},{5,7},{6,4},{7,5},{8,10},{9,11},{10,... | collective-permute-start | bytes 786440 | tf_op jit(solution)/shard_map/ppermute | solution.py:453
  115.4 1.1 collective-permute-start.5
  116.5 6.2 %fold_back.1 = f32[2048,128]{1,0:T(8,128)} custom-call(s32[4096,128]{1,0:T(8,128)} %broadcast_in_dim.29.list_ref, bf16[4096,128]{1,0:T(8,128)(2,1)S(1)} %bitcast.23, f32[2048,128]{1,0:T(8,128)S(1)} %get-tuple-element.31.local_ref), custom_call_target="tpu_custom_call" | custom-call | flops 4294967296 | bytes 16777216 | tf_op jit(solution)/shard_map/fold_back/pallas_call | solution.py:183
  122.7 4.6 %collective-permute-done.4 = bf16[2,4,2,64,128]{4,3,2,1,0:T(8,128)(2,1)S(1)} collective-permute-done((bf16[2,4,2,64,128]{4,3,2,1,0:T(8,128)(2,1)}, bf16[2,4,2,64,128]{4,3,2,1,0:T(8,128)(2,1)S(1)}, u32[]{:S(2)}, u32[]{:S(2)}) %collective-permute-start.4) | collective-permute-done | bytes 262176 | tf_op jit(solution)/shard_map/ppermute | solution.py:453
  127.3 0.9 convert_add_fusion
  (35 shorter events, 0.4 us)
Async XLA Ops:
  0.6 18.7 %copy-start.4 = (f32[36,1024]{1,0:T(8,128)S(1)}, f32[36,1024]{1,0:T(8,128)}, u32[]{:S(2)}) copy-start(f32[36,1024]{1,0:T(8,128)} %param.14) | copy-start | bytes 442372
  1.6 1.0 copy-start
  2.6 16.6 %copy-start.8 = (s32[32]{0:T(128)S(1)}, s32[32]{0:T(128)}, u32[]{:S(2)}) copy-start(s32[32]{0:T(128)} %param.18) | copy-start | bytes 388
  2.6 16.6 %copy-start.7 = (s32[32]{0:T(128)S(1)}, s32[32]{0:T(128)}, u32[]{:S(2)}) copy-start(s32[32]{0:T(128)} %param.20) | copy-start | bytes 388
  7.0 12.9 %copy-start.5 = (bf16[32,3,128]{2,0,1:T(8,128)(2,1)S(1)}, bf16[32,3,128]{2,0,1:T(8,128)(2,1)}, u32[]{:S(2)}) copy-start(bf16[32,3,128]{2,0,1:T(8,128)(2,1)} %param.17) | copy-start | bytes 73732
  7.0 30.9 %all-to-all-start = ((bf16[128,32,128]{2,1,0:T(8,128)(2,1)}), bf16[128,32,128]{2,1,0:T(8,128)(2,1)S(1)}, u32[]{:S(2)}, u32[]{:S(2)}) async-start(bf16[128,32,128]{2,1,0:T(8,128)(2,1)} %bitcast.2), calls=%async_computation | async-start | bytes 2097152 | tf_op jit(solution)/shard_map/all_to_all | solution.py:421
  18.5 4.4 %copy-start.9 = (s32[32]{0:T(128)S(1)}, s32[32]{0:T(128)}, u32[]{:S(2)}) copy-start(s32[32]{0:T(128)} %param.19) | copy-start | bytes 388
  27.5 15.2 %copy-start.6 = (f32[3,4]{1,0:T(4,128)S(1)}, f32[3,4]{1,0:T(4,128)}, u32[]{:S(2)}) copy-start(f32[3,4]{1,0:T(4,128)} %param.21) | copy-start | bytes 148
  27.5 20.9 %copy-start.1 = (bf16[2048,128]{1,0:T(8,128)(2,1)S(1)}, bf16[2048,128]{1,0:T(8,128)(2,1)}, u32[]{:S(2)}) copy-start(bf16[2048,128]{1,0:T(8,128)(2,1)} %x_ref.3) | copy-start | bytes 1572868
  27.5 20.9 %copy-start.2 = (s32[6,1024]{1,0:T(8,128)S(1)}, s32[6,1024]{1,0:T(8,128)}, u32[]{:S(2)}) copy-start(s32[6,1024]{1,0:T(8,128)} %conn_ref.1) | copy-start | bytes 73732
  37.9 46.2 %all-to-all-start.1 = ((bf16[96,136,128]{2,1,0:T(8,128)(2,1)}), bf16[96,136,128]{2,1,0:T(8,128)(2,1)}, u32[]{:S(2)}, u32[]{:S(2)}) async-start(bf16[96,136,128]{2,1,0:T(8,128)(2,1)} %gather_fusion), calls=%async_computation.1 | async-start | bytes 6684672 | tf_op jit(solution)/shard_map/all_to_all | solution.py:432
  42.7 3.7 %collective-permute-start.2 = (f32[3,4]{1,0:T(4,128)S(1)}, f32[3,4]{1,0:T(4,128)S(1)}, u32[]{:S(2)}, u32[]{:S(2)}) collective-permute-start(f32[3,4]{1,0:T(4,128)S(1)} %copy-done.6), channel_id=1, source_target_pairs={{0,1},{1,2},{2,3},{3,0},{4,5},{5,6},{6,7},{7,4},{8,9},{9,10},{10,1... | collective-permute-start | bytes 152 | tf_op jit(solution)/shard_map/ppermute | solution.py:436
  43.2 3.9 %collective-permute-start.1 = (f32[3,4]{1,0:T(4,128)S(1)}, f32[3,4]{1,0:T(4,128)S(1)}, u32[]{:S(2)}, u32[]{:S(2)}) collective-permute-start(f32[3,4]{1,0:T(4,128)S(1)} %copy-done.6), channel_id=1, source_target_pairs={{0,2},{1,3},{2,0},{3,1},{4,6},{5,7},{6,4},{7,5},{8,10},{9,11},{10,... | collective-permute-start | bytes 152 | tf_op jit(solution)/shard_map/ppermute | solution.py:436
  44.8 2.8 %collective-permute-start = (f32[3,4]{1,0:T(4,128)S(1)}, f32[3,4]{1,0:T(4,128)S(1)}, u32[]{:S(2)}, u32[]{:S(2)}) collective-permute-start(f32[3,4]{1,0:T(4,128)S(1)} %copy-done.6), channel_id=1, source_target_pairs={{0,3},{1,0},{2,1},{3,2},{4,7},{5,4},{6,5},{7,6},{8,11},{9,8},{10,9... | collective-permute-start | bytes 152 | tf_op jit(solution)/shard_map/ppermute | solution.py:436
  84.1 32.4 %all-to-all-start.2 = ((bf16[128,32,128]{2,1,0:T(8,128)(2,1)}), bf16[128,32,128]{2,1,0:T(8,128)(2,1)S(1)}, u32[]{:S(2)}, u32[]{:S(2)}) async-start(bf16[128,32,128]{2,1,0:T(8,128)(2,1)} %bitcast.11), calls=%async_computation.2 | async-start | bytes 2097152 | tf_op jit(solution)/shard_map/all_to_all | solution.py:444
  111.3 11.4 %collective-permute-start.3 = (bf16[2,4,2,64,128]{4,3,2,1,0:T(8,128)(2,1)}, bf16[2,4,2,64,128]{4,3,2,1,0:T(8,128)(2,1)S(1)}, u32[]{:S(2)}, u32[]{:S(2)}) collective-permute-start(bf16[2,4,2,64,128]{4,3,2,1,0:T(8,128)(2,1)} %get-tuple-element.34), channel_id=1, source_target_pairs={{0,1},{1,2},{2,3},{3,0},{4,5},{5,6},{6,7},{7,4},{8,9},{9,10},{10,1... | collective-permute-start | bytes 786440 | tf_op jit(solution)/shard_map/ppermute | solution.py:453
  112.8 14.4 %collective-permute-start.4 = (bf16[2,4,2,64,128]{4,3,2,1,0:T(8,128)(2,1)}, bf16[2,4,2,64,128]{4,3,2,1,0:T(8,128)(2,1)S(1)}, u32[]{:S(2)}, u32[]{:S(2)}) collective-permute-start(bf16[2,4,2,64,128]{4,3,2,1,0:T(8,128)(2,1)} %get-tuple-element.35), channel_id=1, source_target_pairs={{0,2},{1,3},{2,0},{3,1},{4,6},{5,7},{6,4},{7,5},{8,10},{9,11},{10,... | collective-permute-start | bytes 786440 | tf_op jit(solution)/shard_map/ppermute | solution.py:453
  115.4 11.9 %collective-permute-start.5 = (bf16[2,4,2,64,128]{4,3,2,1,0:T(8,128)(2,1)}, bf16[2,4,2,64,128]{4,3,2,1,0:T(8,128)(2,1)S(1)}, u32[]{:S(2)}, u32[]{:S(2)}) collective-permute-start(bf16[2,4,2,64,128]{4,3,2,1,0:T(8,128)(2,1)} %get-tuple-element.36), channel_id=1, source_target_pairs={{0,3},{1,0},{2,1},{3,2},{4,7},{5,4},{6,5},{7,6},{8,11},{9,8},{10,9... | collective-permute-start | bytes 786440 | tf_op jit(solution)/shard_map/ppermute | solution.py:453
  116.5 10.8 %copy-start.3 = (f32[2,4,2,64,128]{4,3,2,1,0:T(8,128)S(1)}, f32[2,4,2,64,128]{4,3,2,1,0:T(8,128)}, u32[]{:S(2)}) copy-start(f32[2,4,2,64,128]{4,3,2,1,0:T(8,128)} %get-tuple-element.38) | copy-start | bytes 1572868

commit v4 on v3

--- a/solution.py
+++ b/solution.py
@@ -219,11 +219,9 @@
     return scaled
 
 
-def parent_kernel(arrived_ref, waves_ref, *refs):
-    outs, (blocks_ref, weights_0, sources_0, weights_1, sources_1, sums, landed) = (
-        refs[:-7],
-        refs[-7:],
-    )
+def parent_kernel(arrived_ref, tables_ref, waves_ref, *refs):
+    outs, scratch = refs[:-9], refs[-9:]
+    blocks_ref, spin_ref, weights_0, sources_0, weights_1, sources_1, sums, landed, spun = scratch
     slots, unused, columns = blocks_ref.shape
     cones = waves_ref.shape[1]
     size = columns
@@ -237,6 +235,8 @@
 
     for step in range(steps):
         fetch(step).start()
+    turned = pltpu.make_async_copy(tables_ref, spin_ref, spun)
+    turned.start()
 
     sub = lax.broadcasted_iota(jnp.int32, (8, size), 0)
     y_rows = lax.broadcasted_iota(jnp.int32, (size, columns), 0).astype(jnp.float32)
@@ -315,26 +315,9 @@
 
     lax.fori_loop(0, steps // 2, two, 0)
 
-    node_rows = lax.broadcasted_iota(jnp.int32, (SQUARE, columns), 0)
-
-    def node_value(digit):
-        value = jnp.full((SQUARE, columns), NODE_T[0], jnp.float32)
-        for j in range(1, NODES):
-            value = jnp.where(digit == j, NODE_T[j], value)
-        return value
-
-    nodes = [
-        node_value(node_rows // (NODES * NODES)),
-        node_value(node_rows // NODES % NODES),
-        node_value(node_rows % NODES),
-    ]
+    turned.wait()
     for k in range(cones):
-        turns = None
-        for d in range(3):
-            wave = jnp.broadcast_to(waves_ref[d, k : k + 1, :], (SQUARE, columns))
-            piece = wave * nodes[d]
-            turns = piece if turns is None else turns + piece
-        sine, cosine = sin_cos_turns(2.0 * turns)
+        cosine, sine = spin_ref[k, 0], spin_ref[k, 1]
         base = k * 2 * SQUARE
         out = outs[k // per_dir]
         for p in range(2):
@@ -348,7 +331,7 @@
 SPAN = 8
 
 
-def parent_sums(blocks, waves, dtypes):
+def parent_sums(blocks, tables, waves, dtypes):
     columns = blocks.shape[2]
     cones = waves.shape[1]
     piece = (2, cones // len(dtypes), 2, SQUARE, columns)
@@ -356,16 +339,18 @@
     return pl.pallas_call(
         parent_kernel,
         out_shape=tuple(jax.ShapeDtypeStruct(piece, dtype) for dtype in dtypes),
-        in_specs=[pl.BlockSpec(memory_space=pl.ANY), vmem()],
+        in_specs=[pl.BlockSpec(memory_space=pl.ANY)] * 2 + [vmem()],
         out_specs=(vmem(),) * len(dtypes),
         scratch_shapes=[
             pltpu.VMEM(blocks.shape, blocks.dtype),
+            pltpu.VMEM(tables.shape, tables.dtype),
             pltpu.VMEM((rows, SPAN * columns), jnp.bfloat16),
             pltpu.VMEM((SPAN * columns, 2 * columns), jnp.bfloat16),
             pltpu.VMEM((rows, SPAN * columns), jnp.bfloat16),
             pltpu.VMEM((SPAN * columns, 2 * columns), jnp.bfloat16),
             pltpu.VMEM((rows, 2 * columns), jnp.float32),
             pltpu.SemaphoreType.DMA((blocks.shape[0] // SPAN,)),
+            pltpu.SemaphoreType.DMA,
         ],
         compiler_params=params(60),
         cost_estimate=pl.CostEstimate(
@@ -374,7 +359,7 @@
             transcendentals=0,
         ),
         name="parent_sums",
-    )(blocks, waves)
+    )(blocks, tables, waves)
 
 
 def packed_blocks(currents, positions, block_live, block_owner, block_leaf):
@@ -435,8 +420,14 @@
     for s in range(1, DIRS):
         waves.append(lax.ppermute(cone_waves, "dir", [(i, (i - s) % DIRS) for i in range(DIRS)]))
     waves = jnp.concatenate(waves, axis=1) * (0.5 / math.pi)
+    digits = jnp.arange(SQUARE)[None, :] // jnp.array([[NODES * NODES], [NODES], [1]]) % NODES
+    nodes = jnp.cos((2.0 * digits + 1.0) * (math.pi / (2.0 * NODES)))
+    turns = sum(waves[d][:, None] * nodes[d][None, :] for d in range(3))
+    sine, cosine = sin_cos_turns(2.0 * turns)
+    tables = jnp.stack([cosine, sine], axis=1)[..., None]
+    tables = jnp.broadcast_to(tables, tables.shape[:-1] + (columns,))
     waves = jnp.broadcast_to(waves[:, :, None], waves.shape + (columns,))
-    halo, waves = lax.optimization_barrier((halo, waves))
+    halo, waves, tables = lax.optimization_barrier((halo, waves, tables))
     local, back = element_sums(
         connectivity, x_edges, halo.reshape(partitions * width, columns), mats
     )
@@ -453,7 +444,7 @@
         return lax.ppermute(piece, "dir", [(i, (i + s) % DIRS) for i in range(DIRS)])
 
     half = jnp.bfloat16
-    pieces = parent_sums(arrived, waves, (jnp.float32, half, half, half))
+    pieces = parent_sums(arrived, tables, waves, (jnp.float32, half, half, half))
     moved = [onward(pieces[t], t) for t in range(1, DIRS)]
     interior_out = fold_back(list_lanes, returned.reshape(partitions * width, columns), local)
     interior_out, moved = lax.optimization_barrier((interior_out, moved))

time: 129 us -> 128 us (level)
  waiting for transfers between devices: 30.8 us -> 29.1 us
  local copies, waits for them, and re-layouts: 9.07 us -> 10.4 us
    all_to_all x1, waiting for transfers between devices: 14 us -> 12.2 us  [shards(): lax.all_to_all(packed, 'dom', split_axis=0, concat_axis=0, tiled=True)]
    broadcast_in_dim x0 -> x1, local copies, waits for them, and re-layouts: none -> 1.31 us  [shards(): tables = jnp.broadcast_to(tables, tables.shape[:-1] + (columns,))]
  transfers between devices with their start and end apart: 9 -> 9, of which waited for: 6 -> 6; matrix products, arithmetic and copies ran while one was open for 7% -> 8% of each run, Pallas kernels for 38% -> 38%
where the time goes in v4:
time: 128 us
  Pallas kernels  52.5 us (41%)
  starting transfers between devices  30.9 us (24%)
  waiting for transfers between devices  29.1 us (23%)
  local copies, waits for them, and re-layouts  10.4 us (8%)
  other arithmetic  3.25 us (3%)
  between operations  1.54 us (1%)
    pallas_call x1, Pallas kernels, element_sums(): pl.pallas_call(element_kernel, out_shape=(jax.ShapeDtypeStruct((owned, co...  21.7 us
    pallas_call x1, Pallas kernels, parent_sums(): pl.pallas_call(parent_kernel, out_shape=tuple((jax.ShapeDtypeStruct(piece...  20.2 us
    all_to_all x1, waiting for transfers between devices, shards(): lax.all_to_all(packed, 'dom', split_axis=0, concat_axis=0, tiled=True)  12.2 us
    all_to_all x1, starting transfers between devices, shards(): lax.all_to_all(outgoing, everywhere, split_axis=0, concat_axis=0, tiled=T...  11.5 us
    all_to_all x1, waiting for transfers between devices, shards(): lax.all_to_all(outgoing, everywhere, split_axis=0, concat_axis=0, tiled=T...  10.4 us
    all_to_all x1, starting transfers between devices, shards(): lax.all_to_all(back.reshape(partitions, width, columns), everywhere, spli...  6.47 us
    pallas_call x1, Pallas kernels, fold_back(): pl.pallas_call(fold_kernel, out_shape=jax.ShapeDtypeStruct(local.shape, j...  6.22 us
    ppermute x3, starting transfers between devices, onward(): lax.ppermute(piece, 'dir', [(i, (i + s) % DIRS) for i in range(DIRS)])  5.15 us
  transfers between devices with their start and end apart: 9, of which 6 were waited for; matrix products, arithmetic and copies ran while one was open for 8% of the time, Pallas kernels for 38%

profile of v4, /device:TPU:1, one launch (start us, length us, event | category | flops | bytes accessed | tf_op | source)
XLA Modules:
  0.0 127.7 jit_solution(15223632626447338679)
XLA Ops:
  0.6 0.9 copy.28
  1.6 1.0 copy-done
  2.6 4.3 %pick_rows.1 = bf16[4096,128]{1,0:T(8,128)(2,1)} custom-call(s32[1,4096]{1,0:T(1,128)S(1)} %reshape.542.list_ref, bf16[2048,128]{1,0:T(8,128)(2,1)S(1)} %copy-done), custom_call_target="tpu_custom_call" | custom-call | bytes 16777216 | tf_op jit(solution)/shard_map/pick_rows/pallas_call | solution.py:50
  7.0 11.5 %all-to-all-start = ((bf16[128,32,128]{2,1,0:T(8,128)(2,1)}), bf16[128,32,128]{2,1,0:T(8,128)(2,1)S(1)}, u32[]{:S(2)}, u32[]{:S(2)}) async-start(bf16[128,32,128]{2,1,0:T(8,128)(2,1)} %bitcast.2), calls=%async_computation | async-start | bytes 2097152 | tf_op jit(solution)/shard_map/all_to_all | solution.py:406
  19.3 0.2 copy.29
  19.6 0.2 select_bitcast_fusion.mats_ref
  19.8 0.1 copy.31
  19.9 3.0 %broadcast_in_dim.39.list_ref = s32[4096,128]{1,0:T(8,128)} broadcast(s32[4096]{0:T(1024)S(1)} %broadcast_in_dim.38), dimensions={0} | broadcast | bytes 2113536 | tf_op jit(solution)/shard_map/broadcast_in_dim | solution.py:408
  22.9 0.2 convert_reduce_fusion
  23.3 1.3 %fusion.4 = bf16[33,136,128]{2,1,0:T(8,128)(2,1)S(1)} fusion(bf16[32,5,128]{2,1,0:T(8,128)(2,1)S(1)} %broadcast_in_dim.42, bf16[32,3,128]{2,1,0:T(4,128)(2,1)S(1)} %copy.32, bf16[32,128,128]{2,1,0:T(8,128)(2,1)} %param.17), kind=kLoop, calls=%fused_computation.6 | loop fusion | flops 5744640 | bytes 2263040 | tf_op jit(solution)/shard_map/concatenate | solution.py:374
  24.6 2.9 %gather_fusion = bf16[96,136,128]{2,1,0:T(8,128)(2,1)} fusion(bf16[33,136,128]{2,1,0:T(8,128)(2,1)S(1)} %fusion.4, s32[1024]{0:T(1024)S(1)} %pad_clamp_fusion), kind=kCustom, calls=%fused_computation | custom fusion | bytes 6685056 | tf_op jit(solution)/shard_map/gather | solution.py:383
  27.5 10.4 %all-to-all-done = bf16[128,32,128]{2,1,0:T(8,128)(2,1)S(1)} async-done(((bf16[128,32,128]{2,1,0:T(8,128)(2,1)}), bf16[128,32,128]{2,1,0:T(8,128)(2,1)S(1)}, u32[]{:S(2)}, u32[]{:S(2)}) %all-to-all-start) | async-done | bytes 1048608 | tf_op jit(solution)/shard_map/all_to_all | solution.py:406
  37.9 4.8 %all-to-all-start.1 = ((bf16[96,136,128]{2,1,0:T(8,128)(2,1)}), bf16[96,136,128]{2,1,0:T(8,128)(2,1)}, u32[]{:S(2)}, u32[]{:S(2)}) async-start(bf16[96,136,128]{2,1,0:T(8,128)(2,1)} %gather_fusion), calls=%async_computation.1 | async-start | bytes 6684672 | tf_op jit(solution)/shard_map/all_to_all | solution.py:417
  42.8 0.2 fusion.15
  43.0 0.4 collective-permute-start.2
  43.4 1.7 %collective-permute-start.1 = (f32[3,4]{1,0:T(4,128)S(1)}, f32[3,4]{1,0:T(4,128)S(1)}, u32[]{:S(2)}, u32[]{:S(2)}) collective-permute-start(f32[3,4]{1,0:T(4,128)S(1)} %copy-done.6), channel_id=1, source_target_pairs={{0,2},{1,3},{2,0},{3,1},{4,6},{5,7},{6,4},{7,5},{8,10},{9,11},{10,... | collective-permute-start | bytes 152 | tf_op jit(solution)/shard_map/ppermute | solution.py:421
  45.1 0.9 collective-permute-start
  46.0 1.1 collective-permute-done.2
  47.1 0.2 collective-permute-done.1
  47.4 0.6 collective-permute-done
  48.2 0.7 broadcast_in_dim.45.waves_ref
  48.9 1.3 %broadcast_in_dim.78.tables_ref = f32[16,2,64,128]{3,2,1,0:T(8,128)} broadcast(f32[16,2,64]{2,1,0:T(2,128)S(1)} %copy.33), dimensions={0,1,2} | broadcast | bytes 1056768 | tf_op jit(solution)/shard_map/broadcast_in_dim | solution.py:428
  50.2 21.7 %element_sums.1 = (f32[2048,128]{1,0:T(8,128)S(1)}, bf16[4096,128]{1,0:T(8,128)(2,1)}) custom-call(s32[6,1024]{1,0:T(8,128)S(1)} %copy-done.2, bf16[2048,128]{1,0:T(8,128)(2,1)S(1)} %copy-done.1, bf16[4096,128]{1,0:T(8,128)(2,1)S(1)} %bitcast.34, f32[1024,36]{1,0:T(8,128)S(1)} %select_bitcast_fusion.mats_ref), custom_call_target="tpu_custom_call" | custom-call | bytes 67108864 | tf_op jit(solution)/shard_map/element_sums/pallas_call | solution.py:138
  71.9 12.2 %all-to-all-done.1.arrived_ref = bf16[96,136,128]{2,1,0:T(8,128)(2,1)} async-done(((bf16[96,136,128]{2,1,0:T(8,128)(2,1)}), bf16[96,136,128]{2,1,0:T(8,128)(2,1)}, u32[]{:S(2)}, u32[]{:S(2)}) %all-to-all-start.1) | async-done | bytes 3342368 | tf_op jit(solution)/shard_map/all_to_all | solution.py:417
  84.1 6.5 %all-to-all-start.2 = ((bf16[128,32,128]{2,1,0:T(8,128)(2,1)}), bf16[128,32,128]{2,1,0:T(8,128)(2,1)S(1)}, u32[]{:S(2)}, u32[]{:S(2)}) async-start(bf16[128,32,128]{2,1,0:T(8,128)(2,1)} %bitcast.17), calls=%async_computation.2 | async-start | bytes 2097152 | tf_op jit(solution)/shard_map/all_to_all | solution.py:435
  90.6 20.2 %parent_sums.1 = (f32[2,4,2,64,128]{4,3,2,1,0:T(8,128)}, bf16[2,4,2,64,128]{4,3,2,1,0:T(8,128)(2,1)}, bf16[2,4,2,64,128]{4,3,2,1,0:T(8,128)(2,1)}, bf16[2,4,2,64,128]{4,3,2,1,0:T(8,128)(2,1)}) custom-call(bf16[96,136,128]{2,1,0:T(8,128)(2,1)} %all-to-all-done.1.arrived_ref, f32[16,2,64,128]{3,2,1,0:T(8,128)} %broadcast_in_dim.78.tables_ref, ...), custom_call_target="tpu_custom_call" | custom-call | flops 12884901888 | bytes 8388608 | tf_op jit(solution)/shard_map/parent_sums/pallas_call | solution.py:339
  110.8 1.5 %collective-permute-start.3 = (bf16[2,4,2,64,128]{4,3,2,1,0:T(8,128)(2,1)}, bf16[2,4,2,64,128]{4,3,2,1,0:T(8,128)(2,1)S(1)}, u32[]{:S(2)}, u32[]{:S(2)}) collective-permute-start(bf16[2,4,2,64,128]{4,3,2,1,0:T(8,128)(2,1)} %get-tuple-element.36), channel_id=1, source_target_pairs={{0,1},{1,2},{2,3},{3,0},{4,5},{5,6},{6,7},{7,4},{8,9},{9,10},{10,1... | collective-permute-start | bytes 786440 | tf_op jit(solution)/shard_map/ppermute | solution.py:444
  112.3 2.5 %collective-permute-start.4 = (bf16[2,4,2,64,128]{4,3,2,1,0:T(8,128)(2,1)}, bf16[2,4,2,64,128]{4,3,2,1,0:T(8,128)(2,1)S(1)}, u32[]{:S(2)}, u32[]{:S(2)}) collective-permute-start(bf16[2,4,2,64,128]{4,3,2,1,0:T(8,128)(2,1)} %get-tuple-element.37), channel_id=1, source_target_pairs={{0,2},{1,3},{2,0},{3,1},{4,6},{5,7},{6,4},{7,5},{8,10},{9,11},{10,... | collective-permute-start | bytes 786440 | tf_op jit(solution)/shard_map/ppermute | solution.py:444
  114.9 1.1 collective-permute-start.5
  116.0 6.2 %fold_back.1 = f32[2048,128]{1,0:T(8,128)} custom-call(s32[4096,128]{1,0:T(8,128)} %broadcast_in_dim.39.list_ref, bf16[4096,128]{1,0:T(8,128)(2,1)S(1)} %bitcast.35, f32[2048,128]{1,0:T(8,128)S(1)} %get-tuple-element.32.local_ref), custom_call_target="tpu_custom_call" | custom-call | flops 4294967296 | bytes 16777216 | tf_op jit(solution)/shard_map/fold_back/pallas_call | solution.py:183
  122.2 4.5 %collective-permute-done.4 = bf16[2,4,2,64,128]{4,3,2,1,0:T(8,128)(2,1)S(1)} collective-permute-done((bf16[2,4,2,64,128]{4,3,2,1,0:T(8,128)(2,1)}, bf16[2,4,2,64,128]{4,3,2,1,0:T(8,128)(2,1)S(1)}, u32[]{:S(2)}, u32[]{:S(2)}) %collective-permute-start.4) | collective-permute-done | bytes 262176 | tf_op jit(solution)/shard_map/ppermute | solution.py:444
  126.8 0.9 convert_add_fusion
  (45 shorter events, 0.7 us)
Async XLA Ops:
  0.6 18.7 %copy-start.4 = (f32[36,1024]{1,0:T(8,128)S(1)}, f32[36,1024]{1,0:T(8,128)}, u32[]{:S(2)}) copy-start(f32[36,1024]{1,0:T(8,128)} %param.15) | copy-start | bytes 442372
  1.6 1.0 copy-start
  2.6 16.6 %copy-start.9 = (s32[32]{0:T(128)S(1)}, s32[32]{0:T(128)}, u32[]{:S(2)}) copy-start(s32[32]{0:T(128)} %param.19) | copy-start | bytes 388
  2.6 16.6 %copy-start.7 = (s32[32]{0:T(128)S(1)}, s32[32]{0:T(128)}, u32[]{:S(2)}) copy-start(s32[32]{0:T(128)} %param.21) | copy-start | bytes 388
  7.0 12.9 %copy-start.5 = (bf16[32,3,128]{2,0,1:T(8,128)(2,1)S(1)}, bf16[32,3,128]{2,0,1:T(8,128)(2,1)}, u32[]{:S(2)}) copy-start(bf16[32,3,128]{2,0,1:T(8,128)(2,1)} %param.18) | copy-start | bytes 73732
  7.0 30.9 %all-to-all-start = ((bf16[128,32,128]{2,1,0:T(8,128)(2,1)}), bf16[128,32,128]{2,1,0:T(8,128)(2,1)S(1)}, u32[]{:S(2)}, u32[]{:S(2)}) async-start(bf16[128,32,128]{2,1,0:T(8,128)(2,1)} %bitcast.2), calls=%async_computation | async-start | bytes 2097152 | tf_op jit(solution)/shard_map/all_to_all | solution.py:406
  18.5 4.4 %copy-start.10 = (s32[32]{0:T(128)S(1)}, s32[32]{0:T(128)}, u32[]{:S(2)}) copy-start(s32[32]{0:T(128)} %param.20) | copy-start | bytes 388
  27.5 15.2 %copy-start.8 = (s32[3]{0:T(128)S(1)}, s32[3]{0:T(128)}, u32[]{:S(2)}) copy-start(s32[3]{0:T(128)} %constant.142) | copy-start | bytes 40
  27.5 15.5 %copy-start.6 = (f32[3,4]{1,0:T(4,128)S(1)}, f32[3,4]{1,0:T(4,128)}, u32[]{:S(2)}) copy-start(f32[3,4]{1,0:T(4,128)} %param.22) | copy-start | bytes 148
  27.5 22.7 %copy-start.1 = (bf16[2048,128]{1,0:T(8,128)(2,1)S(1)}, bf16[2048,128]{1,0:T(8,128)(2,1)}, u32[]{:S(2)}) copy-start(bf16[2048,128]{1,0:T(8,128)(2,1)} %x_ref.3) | copy-start | bytes 1572868
  27.5 22.7 %copy-start.2 = (s32[6,1024]{1,0:T(8,128)S(1)}, s32[6,1024]{1,0:T(8,128)}, u32[]{:S(2)}) copy-start(s32[6,1024]{1,0:T(8,128)} %conn_ref.1) | copy-start | bytes 73732
  37.9 46.2 %all-to-all-start.1 = ((bf16[96,136,128]{2,1,0:T(8,128)(2,1)}), bf16[96,136,128]{2,1,0:T(8,128)(2,1)}, u32[]{:S(2)}, u32[]{:S(2)}) async-start(bf16[96,136,128]{2,1,0:T(8,128)(2,1)} %gather_fusion), calls=%async_computation.1 | async-start | bytes 6684672 | tf_op jit(solution)/shard_map/all_to_all | solution.py:417
  43.0 4.1 %collective-permute-start.2 = (f32[3,4]{1,0:T(4,128)S(1)}, f32[3,4]{1,0:T(4,128)S(1)}, u32[]{:S(2)}, u32[]{:S(2)}) collective-permute-start(f32[3,4]{1,0:T(4,128)S(1)} %copy-done.6), channel_id=1, source_target_pairs={{0,1},{1,2},{2,3},{3,0},{4,5},{5,6},{6,7},{7,4},{8,9},{9,10},{10,1... | collective-permute-start | bytes 152 | tf_op jit(solution)/shard_map/ppermute | solution.py:421
  43.4 3.9 %collective-permute-start.1 = (f32[3,4]{1,0:T(4,128)S(1)}, f32[3,4]{1,0:T(4,128)S(1)}, u32[]{:S(2)}, u32[]{:S(2)}) collective-permute-start(f32[3,4]{1,0:T(4,128)S(1)} %copy-done.6), channel_id=1, source_target_pairs={{0,2},{1,3},{2,0},{3,1},{4,6},{5,7},{6,4},{7,5},{8,10},{9,11},{10,... | collective-permute-start | bytes 152 | tf_op jit(solution)/shard_map/ppermute | solution.py:421
  45.1 2.8 %collective-permute-start = (f32[3,4]{1,0:T(4,128)S(1)}, f32[3,4]{1,0:T(4,128)S(1)}, u32[]{:S(2)}, u32[]{:S(2)}) collective-permute-start(f32[3,4]{1,0:T(4,128)S(1)} %copy-done.6), channel_id=1, source_target_pairs={{0,3},{1,0},{2,1},{3,2},{4,7},{5,4},{6,5},{7,6},{8,11},{9,8},{10,9... | collective-permute-start | bytes 152 | tf_op jit(solution)/shard_map/ppermute | solution.py:421
  84.1 31.9 %all-to-all-start.2 = ((bf16[128,32,128]{2,1,0:T(8,128)(2,1)}), bf16[128,32,128]{2,1,0:T(8,128)(2,1)S(1)}, u32[]{:S(2)}, u32[]{:S(2)}) async-start(bf16[128,32,128]{2,1,0:T(8,128)(2,1)} %bitcast.17), calls=%async_computation.2 | async-start | bytes 2097152 | tf_op jit(solution)/shard_map/all_to_all | solution.py:435
  110.8 11.4 %collective-permute-start.3 = (bf16[2,4,2,64,128]{4,3,2,1,0:T(8,128)(2,1)}, bf16[2,4,2,64,128]{4,3,2,1,0:T(8,128)(2,1)S(1)}, u32[]{:S(2)}, u32[]{:S(2)}) collective-permute-start(bf16[2,4,2,64,128]{4,3,2,1,0:T(8,128)(2,1)} %get-tuple-element.36), channel_id=1, source_target_pairs={{0,1},{1,2},{2,3},{3,0},{4,5},{5,6},{6,7},{7,4},{8,9},{9,10},{10,1... | collective-permute-start | bytes 786440 | tf_op jit(solution)/shard_map/ppermute | solution.py:444
  112.3 14.4 %collective-permute-start.4 = (bf16[2,4,2,64,128]{4,3,2,1,0:T(8,128)(2,1)}, bf16[2,4,2,64,128]{4,3,2,1,0:T(8,128)(2,1)S(1)}, u32[]{:S(2)}, u32[]{:S(2)}) collective-permute-start(bf16[2,4,2,64,128]{4,3,2,1,0:T(8,128)(2,1)} %get-tuple-element.37), channel_id=1, source_target_pairs={{0,2},{1,3},{2,0},{3,1},{4,6},{5,7},{6,4},{7,5},{8,10},{9,11},{10,... | collective-permute-start | bytes 786440 | tf_op jit(solution)/shard_map/ppermute | solution.py:444
  114.9 11.9 %collective-permute-start.5 = (bf16[2,4,2,64,128]{4,3,2,1,0:T(8,128)(2,1)}, bf16[2,4,2,64,128]{4,3,2,1,0:T(8,128)(2,1)S(1)}, u32[]{:S(2)}, u32[]{:S(2)}) collective-permute-start(bf16[2,4,2,64,128]{4,3,2,1,0:T(8,128)(2,1)} %get-tuple-element.38), channel_id=1, source_target_pairs={{0,3},{1,0},{2,1},{3,2},{4,7},{5,4},{6,5},{7,6},{8,11},{9,8},{10,9... | collective-permute-start | bytes 786440 | tf_op jit(solution)/shard_map/ppermute | solution.py:444
  116.0 10.8 %copy-start.3 = (f32[2,4,2,64,128]{4,3,2,1,0:T(8,128)S(1)}, f32[2,4,2,64,128]{4,3,2,1,0:T(8,128)}, u32[]{:S(2)}) copy-start(f32[2,4,2,64,128]{4,3,2,1,0:T(8,128)} %get-tuple-element.40) | copy-start | bytes 1572868

commit v5 on v4

--- a/solution.py
+++ b/solution.py
@@ -284,7 +284,7 @@
                 basis * jnp.broadcast_to(-sine[k : k + 1, :], (SQUARE, size))
             ).astype(jnp.bfloat16)
 
-    height = min(512, cones * 2 * SQUARE)
+    height = min(1024, cones * 2 * SQUARE)
     chunks = cones * 2 * SQUARE // height
     share = max(1, span // chunks)
 
@@ -445,7 +445,7 @@
 
     half = jnp.bfloat16
     pieces = parent_sums(arrived, tables, waves, (jnp.float32, half, half, half))
-    moved = [onward(pieces[t], t) for t in range(1, DIRS)]
+    moved = [onward(pieces[t], t) for t in (2, 1, 3)]
     interior_out = fold_back(list_lanes, returned.reshape(partitions * width, columns), local)
     interior_out, moved = lax.optimization_barrier((interior_out, moved))
     expansions = pieces[0]

time: 128 us -> 128 us (level)
  no operation moved by 1% of the time
where the time goes in v5:
time: 128 us; the launch traced here: 127 us
  Pallas kernels  52.3 us (41%)
  starting transfers between devices  31.5 us (25%)
  waiting for transfers between devices  28.3 us (22%)
  local copies, waits for them, and re-layouts  10.4 us (8%)
  other arithmetic  3.25 us (3%)
  between operations  1.54 us (1%)
    pallas_call x1, Pallas kernels, element_sums(): pl.pallas_call(element_kernel, out_shape=(jax.ShapeDtypeStruct((owned, co...  21.7 us
    pallas_call x1, Pallas kernels, parent_sums(): pl.pallas_call(parent_kernel, out_shape=tuple((jax.ShapeDtypeStruct(piece...  20 us
    all_to_all x1, waiting for transfers between devices, shards(): lax.all_to_all(packed, 'dom', split_axis=0, concat_axis=0, tiled=True)  12.2 us
    all_to_all x1, starting transfers between devices, shards(): lax.all_to_all(outgoing, everywhere, split_axis=0, concat_axis=0, tiled=T...  11.5 us
    all_to_all x1, waiting for transfers between devices, shards(): lax.all_to_all(outgoing, everywhere, split_axis=0, concat_axis=0, tiled=T...  10.4 us
    all_to_all x1, starting transfers between devices, shards(): lax.all_to_all(back.reshape(partitions, width, columns), everywhere, spli...  6.47 us
    pallas_call x1, Pallas kernels, fold_back(): pl.pallas_call(fold_kernel, out_shape=jax.ShapeDtypeStruct(local.shape, j...  6.22 us
    ppermute x3, starting transfers between devices, onward(): lax.ppermute(piece, 'dir', [(i, (i + s) % DIRS) for i in range(DIRS)])  5.77 us
  transfers between devices with their start and end apart: 9, of which 6 were waited for; matrix products, arithmetic and copies ran while one was open for 8% of the time, Pallas kernels for 38%

profile of v5, /device:TPU:1, one launch (start us, length us, event | category | flops | bytes accessed | tf_op | source)
XLA Modules:
  0.0 127.3 jit_solution(11247455276738550884)
XLA Ops:
  0.6 0.9 copy.28
  1.6 1.0 copy-done
  2.6 4.3 %pick_rows.1 = bf16[4096,128]{1,0:T(8,128)(2,1)} custom-call(s32[1,4096]{1,0:T(1,128)S(1)} %reshape.542.list_ref, bf16[2048,128]{1,0:T(8,128)(2,1)S(1)} %copy-done), custom_call_target="tpu_custom_call" | custom-call | bytes 16777216 | tf_op jit(solution)/shard_map/pick_rows/pallas_call | solution.py:50
  7.0 11.5 %all-to-all-start = ((bf16[128,32,128]{2,1,0:T(8,128)(2,1)}), bf16[128,32,128]{2,1,0:T(8,128)(2,1)S(1)}, u32[]{:S(2)}, u32[]{:S(2)}) async-start(bf16[128,32,128]{2,1,0:T(8,128)(2,1)} %bitcast.2), calls=%async_computation | async-start | bytes 2097152 | tf_op jit(solution)/shard_map/all_to_all | solution.py:406
  19.3 0.2 copy.29
  19.6 0.2 select_bitcast_fusion.mats_ref
  19.8 0.1 copy.31
  19.9 3.0 %broadcast_in_dim.39.list_ref = s32[4096,128]{1,0:T(8,128)} broadcast(s32[4096]{0:T(1024)S(1)} %broadcast_in_dim.38), dimensions={0} | broadcast | bytes 2113536 | tf_op jit(solution)/shard_map/broadcast_in_dim | solution.py:408
  22.9 0.2 convert_reduce_fusion
  23.3 1.3 %fusion.4 = bf16[33,136,128]{2,1,0:T(8,128)(2,1)S(1)} fusion(bf16[32,5,128]{2,1,0:T(8,128)(2,1)S(1)} %broadcast_in_dim.42, bf16[32,3,128]{2,1,0:T(4,128)(2,1)S(1)} %copy.32, bf16[32,128,128]{2,1,0:T(8,128)(2,1)} %param.17), kind=kLoop, calls=%fused_computation.6 | loop fusion | flops 5744640 | bytes 2263040 | tf_op jit(solution)/shard_map/concatenate | solution.py:374
  24.6 2.9 %gather_fusion = bf16[96,136,128]{2,1,0:T(8,128)(2,1)} fusion(bf16[33,136,128]{2,1,0:T(8,128)(2,1)S(1)} %fusion.4, s32[1024]{0:T(1024)S(1)} %pad_clamp_fusion), kind=kCustom, calls=%fused_computation | custom fusion | bytes 6685056 | tf_op jit(solution)/shard_map/gather | solution.py:383
  27.5 10.4 %all-to-all-done = bf16[128,32,128]{2,1,0:T(8,128)(2,1)S(1)} async-done(((bf16[128,32,128]{2,1,0:T(8,128)(2,1)}), bf16[128,32,128]{2,1,0:T(8,128)(2,1)S(1)}, u32[]{:S(2)}, u32[]{:S(2)}) %all-to-all-start) | async-done | bytes 1048608 | tf_op jit(solution)/shard_map/all_to_all | solution.py:406
  37.9 4.8 %all-to-all-start.1 = ((bf16[96,136,128]{2,1,0:T(8,128)(2,1)}), bf16[96,136,128]{2,1,0:T(8,128)(2,1)}, u32[]{:S(2)}, u32[]{:S(2)}) async-start(bf16[96,136,128]{2,1,0:T(8,128)(2,1)} %gather_fusion), calls=%async_computation.1 | async-start | bytes 6684672 | tf_op jit(solution)/shard_map/all_to_all | solution.py:417
  42.8 0.2 fusion.15
  43.0 0.4 collective-permute-start.2
  43.4 1.7 %collective-permute-start.1 = (f32[3,4]{1,0:T(4,128)S(1)}, f32[3,4]{1,0:T(4,128)S(1)}, u32[]{:S(2)}, u32[]{:S(2)}) collective-permute-start(f32[3,4]{1,0:T(4,128)S(1)} %copy-done.6), channel_id=1, source_target_pairs={{0,2},{1,3},{2,0},{3,1},{4,6},{5,7},{6,4},{7,5},{8,10},{9,11},{10,... | collective-permute-start | bytes 152 | tf_op jit(solution)/shard_map/ppermute | solution.py:421
  45.1 0.9 collective-permute-start
  46.0 1.1 collective-permute-done.2
  47.1 0.2 collective-permute-done.1
  47.4 0.6 collective-permute-done
  48.2 0.7 broadcast_in_dim.45.waves_ref
  48.9 1.3 %broadcast_in_dim.78.tables_ref = f32[16,2,64,128]{3,2,1,0:T(8,128)} broadcast(f32[16,2,64]{2,1,0:T(2,128)S(1)} %copy.33), dimensions={0,1,2} | broadcast | bytes 1056768 | tf_op jit(solution)/shard_map/broadcast_in_dim | solution.py:428
  50.2 21.7 %element_sums.1 = (f32[2048,128]{1,0:T(8,128)S(1)}, bf16[4096,128]{1,0:T(8,128)(2,1)}) custom-call(s32[6,1024]{1,0:T(8,128)S(1)} %copy-done.2, bf16[2048,128]{1,0:T(8,128)(2,1)S(1)} %copy-done.1, bf16[4096,128]{1,0:T(8,128)(2,1)S(1)} %bitcast.34, f32[1024,36]{1,0:T(8,128)S(1)} %select_bitcast_fusion.mats_ref), custom_call_target="tpu_custom_call" | custom-call | bytes 67108864 | tf_op jit(solution)/shard_map/element_sums/pallas_call | solution.py:138
  71.9 12.2 %all-to-all-done.1.arrived_ref = bf16[96,136,128]{2,1,0:T(8,128)(2,1)} async-done(((bf16[96,136,128]{2,1,0:T(8,128)(2,1)}), bf16[96,136,128]{2,1,0:T(8,128)(2,1)}, u32[]{:S(2)}, u32[]{:S(2)}) %all-to-all-start.1) | async-done | bytes 3342368 | tf_op jit(solution)/shard_map/all_to_all | solution.py:417
  84.1 6.5 %all-to-all-start.2 = ((bf16[128,32,128]{2,1,0:T(8,128)(2,1)}), bf16[128,32,128]{2,1,0:T(8,128)(2,1)S(1)}, u32[]{:S(2)}, u32[]{:S(2)}) async-start(bf16[128,32,128]{2,1,0:T(8,128)(2,1)} %bitcast.17), calls=%async_computation.2 | async-start | bytes 2097152 | tf_op jit(solution)/shard_map/all_to_all | solution.py:435
  90.6 20.0 %parent_sums.1 = (f32[2,4,2,64,128]{4,3,2,1,0:T(8,128)}, bf16[2,4,2,64,128]{4,3,2,1,0:T(8,128)(2,1)}, bf16[2,4,2,64,128]{4,3,2,1,0:T(8,128)(2,1)}, bf16[2,4,2,64,128]{4,3,2,1,0:T(8,128)(2,1)}) custom-call(bf16[96,136,128]{2,1,0:T(8,128)(2,1)} %all-to-all-done.1.arrived_ref, f32[16,2,64,128]{3,2,1,0:T(8,128)} %broadcast_in_dim.78.tables_ref, ...), custom_call_target="tpu_custom_call" | custom-call | flops 12884901888 | bytes 8388608 | tf_op jit(solution)/shard_map/parent_sums/pallas_call | solution.py:339
  110.6 3.1 %collective-permute-start.3 = (bf16[2,4,2,64,128]{4,3,2,1,0:T(8,128)(2,1)}, bf16[2,4,2,64,128]{4,3,2,1,0:T(8,128)(2,1)S(1)}, u32[]{:S(2)}, u32[]{:S(2)}) collective-permute-start(bf16[2,4,2,64,128]{4,3,2,1,0:T(8,128)(2,1)} %get-tuple-element.36), channel_id=1, source_target_pairs={{0,2},{1,3},{2,0},{3,1},{4,6},{5,7},{6,4},{7,5},{8,10},{9,11},{10,... | collective-permute-start | bytes 786440 | tf_op jit(solution)/shard_map/ppermute | solution.py:444
  113.7 0.4 collective-permute-start.4
  114.1 2.3 %collective-permute-start.5 = (bf16[2,4,2,64,128]{4,3,2,1,0:T(8,128)(2,1)}, bf16[2,4,2,64,128]{4,3,2,1,0:T(8,128)(2,1)S(1)}, u32[]{:S(2)}, u32[]{:S(2)}) collective-permute-start(bf16[2,4,2,64,128]{4,3,2,1,0:T(8,128)(2,1)} %get-tuple-element.38), channel_id=1, source_target_pairs={{0,3},{1,0},{2,1},{3,2},{4,7},{5,4},{6,5},{7,6},{8,11},{9,8},{10,9... | collective-permute-start | bytes 786440 | tf_op jit(solution)/shard_map/ppermute | solution.py:444
  116.4 6.2 %fold_back.1 = f32[2048,128]{1,0:T(8,128)} custom-call(s32[4096,128]{1,0:T(8,128)} %broadcast_in_dim.39.list_ref, bf16[4096,128]{1,0:T(8,128)(2,1)S(1)} %bitcast.35, f32[2048,128]{1,0:T(8,128)S(1)} %get-tuple-element.32.local_ref), custom_call_target="tpu_custom_call" | custom-call | flops 4294967296 | bytes 16777216 | tf_op jit(solution)/shard_map/fold_back/pallas_call | solution.py:183
  122.6 3.7 %collective-permute-done.4 = bf16[2,4,2,64,128]{4,3,2,1,0:T(8,128)(2,1)S(1)} collective-permute-done((bf16[2,4,2,64,128]{4,3,2,1,0:T(8,128)(2,1)}, bf16[2,4,2,64,128]{4,3,2,1,0:T(8,128)(2,1)S(1)}, u32[]{:S(2)}, u32[]{:S(2)}) %collective-permute-start.4) | collective-permute-done | bytes 262176 | tf_op jit(solution)/shard_map/ppermute | solution.py:444
  126.3 0.9 convert_add_fusion
  (45 shorter events, 0.7 us)
Async XLA Ops:
  0.6 18.7 %copy-start.4 = (f32[36,1024]{1,0:T(8,128)S(1)}, f32[36,1024]{1,0:T(8,128)}, u32[]{:S(2)}) copy-start(f32[36,1024]{1,0:T(8,128)} %param.15) | copy-start | bytes 442372
  1.6 1.0 copy-start
  2.6 16.6 %copy-start.9 = (s32[32]{0:T(128)S(1)}, s32[32]{0:T(128)}, u32[]{:S(2)}) copy-start(s32[32]{0:T(128)} %param.19) | copy-start | bytes 388
  2.6 16.6 %copy-start.7 = (s32[32]{0:T(128)S(1)}, s32[32]{0:T(128)}, u32[]{:S(2)}) copy-start(s32[32]{0:T(128)} %param.21) | copy-start | bytes 388
  7.0 12.9 %copy-start.5 = (bf16[32,3,128]{2,0,1:T(8,128)(2,1)S(1)}, bf16[32,3,128]{2,0,1:T(8,128)(2,1)}, u32[]{:S(2)}) copy-start(bf16[32,3,128]{2,0,1:T(8,128)(2,1)} %param.18) | copy-start | bytes 73732
  7.0 30.9 %all-to-all-start = ((bf16[128,32,128]{2,1,0:T(8,128)(2,1)}), bf16[128,32,128]{2,1,0:T(8,128)(2,1)S(1)}, u32[]{:S(2)}, u32[]{:S(2)}) async-start(bf16[128,32,128]{2,1,0:T(8,128)(2,1)} %bitcast.2), calls=%async_computation | async-start | bytes 2097152 | tf_op jit(solution)/shard_map/all_to_all | solution.py:406
  18.5 4.4 %copy-start.10 = (s32[32]{0:T(128)S(1)}, s32[32]{0:T(128)}, u32[]{:S(2)}) copy-start(s32[32]{0:T(128)} %param.20) | copy-start | bytes 388
  27.5 15.2 %copy-start.8 = (s32[3]{0:T(128)S(1)}, s32[3]{0:T(128)}, u32[]{:S(2)}) copy-start(s32[3]{0:T(128)} %constant.142) | copy-start | bytes 40
  27.5 15.5 %copy-start.6 = (f32[3,4]{1,0:T(4,128)S(1)}, f32[3,4]{1,0:T(4,128)}, u32[]{:S(2)}) copy-start(f32[3,4]{1,0:T(4,128)} %param.22) | copy-start | bytes 148
  27.5 22.7 %copy-start.1 = (bf16[2048,128]{1,0:T(8,128)(2,1)S(1)}, bf16[2048,128]{1,0:T(8,128)(2,1)}, u32[]{:S(2)}) copy-start(bf16[2048,128]{1,0:T(8,128)(2,1)} %x_ref.3) | copy-start | bytes 1572868
  27.5 22.7 %copy-start.2 = (s32[6,1024]{1,0:T(8,128)S(1)}, s32[6,1024]{1,0:T(8,128)}, u32[]{:S(2)}) copy-start(s32[6,1024]{1,0:T(8,128)} %conn_ref.1) | copy-start | bytes 73732
  37.9 46.2 %all-to-all-start.1 = ((bf16[96,136,128]{2,1,0:T(8,128)(2,1)}), bf16[96,136,128]{2,1,0:T(8,128)(2,1)}, u32[]{:S(2)}, u32[]{:S(2)}) async-start(bf16[96,136,128]{2,1,0:T(8,128)(2,1)} %gather_fusion), calls=%async_computation.1 | async-start | bytes 6684672 | tf_op jit(solution)/shard_map/all_to_all | solution.py:417
  43.0 4.1 %collective-permute-start.2 = (f32[3,4]{1,0:T(4,128)S(1)}, f32[3,4]{1,0:T(4,128)S(1)}, u32[]{:S(2)}, u32[]{:S(2)}) collective-permute-start(f32[3,4]{1,0:T(4,128)S(1)} %copy-done.6), channel_id=1, source_target_pairs={{0,1},{1,2},{2,3},{3,0},{4,5},{5,6},{6,7},{7,4},{8,9},{9,10},{10,1... | collective-permute-start | bytes 152 | tf_op jit(solution)/shard_map/ppermute | solution.py:421
  43.4 3.9 %collective-permute-start.1 = (f32[3,4]{1,0:T(4,128)S(1)}, f32[3,4]{1,0:T(4,128)S(1)}, u32[]{:S(2)}, u32[]{:S(2)}) collective-permute-start(f32[3,4]{1,0:T(4,128)S(1)} %copy-done.6), channel_id=1, source_target_pairs={{0,2},{1,3},{2,0},{3,1},{4,6},{5,7},{6,4},{7,5},{8,10},{9,11},{10,... | collective-permute-start | bytes 152 | tf_op jit(solution)/shard_map/ppermute | solution.py:421
  45.1 2.8 %collective-permute-start = (f32[3,4]{1,0:T(4,128)S(1)}, f32[3,4]{1,0:T(4,128)S(1)}, u32[]{:S(2)}, u32[]{:S(2)}) collective-permute-start(f32[3,4]{1,0:T(4,128)S(1)} %copy-done.6), channel_id=1, source_target_pairs={{0,3},{1,0},{2,1},{3,2},{4,7},{5,4},{6,5},{7,6},{8,11},{9,8},{10,9... | collective-permute-start | bytes 152 | tf_op jit(solution)/shard_map/ppermute | solution.py:421
  84.1 32.3 %all-to-all-start.2 = ((bf16[128,32,128]{2,1,0:T(8,128)(2,1)}), bf16[128,32,128]{2,1,0:T(8,128)(2,1)S(1)}, u32[]{:S(2)}, u32[]{:S(2)}) async-start(bf16[128,32,128]{2,1,0:T(8,128)(2,1)} %bitcast.17), calls=%async_computation.2 | async-start | bytes 2097152 | tf_op jit(solution)/shard_map/all_to_all | solution.py:435
  110.6 12.0 %collective-permute-start.3 = (bf16[2,4,2,64,128]{4,3,2,1,0:T(8,128)(2,1)}, bf16[2,4,2,64,128]{4,3,2,1,0:T(8,128)(2,1)S(1)}, u32[]{:S(2)}, u32[]{:S(2)}) collective-permute-start(bf16[2,4,2,64,128]{4,3,2,1,0:T(8,128)(2,1)} %get-tuple-element.36), channel_id=1, source_target_pairs={{0,2},{1,3},{2,0},{3,1},{4,6},{5,7},{6,4},{7,5},{8,10},{9,11},{10,... | collective-permute-start | bytes 786440 | tf_op jit(solution)/shard_map/ppermute | solution.py:444
  113.7 12.6 %collective-permute-start.4 = (bf16[2,4,2,64,128]{4,3,2,1,0:T(8,128)(2,1)}, bf16[2,4,2,64,128]{4,3,2,1,0:T(8,128)(2,1)S(1)}, u32[]{:S(2)}, u32[]{:S(2)}) collective-permute-start(bf16[2,4,2,64,128]{4,3,2,1,0:T(8,128)(2,1)} %get-tuple-element.37), channel_id=1, source_target_pairs={{0,1},{1,2},{2,3},{3,0},{4,5},{5,6},{6,7},{7,4},{8,9},{9,10},{10,1... | collective-permute-start | bytes 786440 | tf_op jit(solution)/shard_map/ppermute | solution.py:444
  114.1 12.2 %collective-permute-start.5 = (bf16[2,4,2,64,128]{4,3,2,1,0:T(8,128)(2,1)}, bf16[2,4,2,64,128]{4,3,2,1,0:T(8,128)(2,1)S(1)}, u32[]{:S(2)}, u32[]{:S(2)}) collective-permute-start(bf16[2,4,2,64,128]{4,3,2,1,0:T(8,128)(2,1)} %get-tuple-element.38), channel_id=1, source_target_pairs={{0,3},{1,0},{2,1},{3,2},{4,7},{5,4},{6,5},{7,6},{8,11},{9,8},{10,9... | collective-permute-start | bytes 786440 | tf_op jit(solution)/shard_map/ppermute | solution.py:444
  116.4 9.9 %copy-start.3 = (f32[2,4,2,64,128]{4,3,2,1,0:T(8,128)S(1)}, f32[2,4,2,64,128]{4,3,2,1,0:T(8,128)}, u32[]{:S(2)}) copy-start(f32[2,4,2,64,128]{4,3,2,1,0:T(8,128)} %get-tuple-element.40) | copy-start | bytes 1572868
